TPU v7x, 32 devices: a whole 2x2x4 slice. The times are simulated.
32 devices in a mesh: group: 2 (over x), region: 8 (over z, y), window: 2 (over core).
Axes of the slice: x: 2, y: 2, z: 4, core: 2. Of those that a mesh axis runs over, the one named last changes fastest.
Arguments:
- flux: bfloat16 [32, 4096, 128], P(('group', 'window'), 'region'), parts along dimension 0, may hold values from -6 to 6
- blend: float32 [16, 16], replicated
- footprints: bfloat16 [4, 8192, 4096], P(('group', 'window'), 'region'), parts along dimension 0, may hold values from -0.03125 to 0.03125
- receptor_block: int32 [4, 8192], P(('group', 'window'), 'region'), parts along dimension 0, may hold values from 0 to 15, as said below
- cell_block: int32 [4, 8192], P(('group', 'window'), 'region'), parts along dimension 0, may hold values from 0 to 7
- slice_index: int32 [4, 8192], P(('group', 'window'), 'region'), parts along dimension 0, may hold values from 0 to 15
- live_counts: int32 [4, 8], P(('group', 'window'), 'region'), parts along dimension 0, may hold values from 16 to 1024, as said below
- observed: bfloat16 [4, 1024, 128], P(('group', 'window'), 'region'), parts along dimension 0, may hold values from -3 to 3
- inv_var: float32 [4, 1024], P(('group', 'window'), 'region'), parts along dimension 0, may hold values from 0.5 to 2
- prior_mix: bfloat16 [128, 128], replicated, may hold values from -2 to 2
Outputs:
- misfit: bfloat16 [4, 1024, 128], P(('group', 'window'), 'region'), parts along dimension 0
- gradient: bfloat16 [32, 4096, 128], P(('group', 'window'), 'region'), parts along dimension 0
There are 2 independent parts, one for each index of `group`. A program takes and returns all parts, laid end to end along the dimension named above; an argument that names none is the same for every part. Nothing has to cross between parts.
Inputs may be any that keep to these rules, and one draw needn't show every extreme that they name: `receptor_block`: receptor blocks j * 2 to (j + 1) * 2 - 1 of a window belong to region j. Of the 1024 slots of one window and region, the first live_counts entries are footprint blocks and the rest are unused. The live blocks of one window and region name at most 2 distinct receptor blocks of any one region, and in every draw, for each window, some region has 2 of its receptor blocks named by the live blocks of every region. `live_counts`: some window and region has all 1024 slots live.
All inputs are finite; a program needn't handle non-finite values.
Results may differ from a plain program's by a relative error of at most 0.018.
Values may be sent and summed in bfloat16 or wider, within the bound.
A program may use at most 192 MiB of HBM per device.

v0:
```python
import jax
import jax.numpy as jnp
from jax import lax
from jax.sharding import PartitionSpec as P

BLOCK = 64


def grouped_sum(values, labels, first_label, label_count):
    shifted = labels - first_label
    table = (shifted[:, None] == jnp.arange(label_count)[None, :]).astype(jnp.bfloat16)
    high_part = values.astype(jnp.bfloat16)
    low_part = (values - high_part.astype(jnp.float32)).astype(jnp.bfloat16)
    upper = jnp.einsum("kl,kd->ld", table, high_part, preferred_element_type=jnp.float32)
    lower = jnp.einsum("kl,kd->ld", table, low_part, preferred_element_type=jnp.float32)
    return upper + lower


def pick_rows(source, labels):
    table = (labels[:, None] == jnp.arange(source.shape[0])[None, :]).astype(source.dtype)
    return jnp.einsum("kp,pbe->kbe", table, source, preferred_element_type=jnp.float32).astype(
        source.dtype
    )


def shards(
    flux,
    blend,
    footprints,
    receptor_block,
    cell_block,
    slice_index,
    live_counts,
    observed,
    inv_var,
    prior_mix,
):
    highest = lax.Precision.HIGHEST
    regions = lax.axis_size("region")
    slab_count, cells_here, ens_width = flux.shape
    slice_total = blend.shape[0]
    cell_blocks = cells_here // BLOCK
    block_slots = footprints.shape[1]
    own_blocks = observed.shape[1] // BLOCK
    window_blocks = own_blocks * regions
    weights = blend
    blended = jnp.einsum(
        "ts,sce->tce",
        weights,
        lax.all_gather(flux, "window", axis=0, tiled=True).astype(jnp.float32),
        precision=highest,
    ).astype(jnp.bfloat16)
    panels = blended.reshape(slice_total * cell_blocks, BLOCK, ens_width)
    footprint = footprints[0].reshape(block_slots, BLOCK, BLOCK)
    receptor_ids = receptor_block[0]
    panel_ids = slice_index[0] * cell_blocks + cell_block[0]
    live_mask = jnp.arange(block_slots) < live_counts[0, 0]
    products = jnp.einsum(
        "kab,kbe->kae", footprint, pick_rows(panels, panel_ids), preferred_element_type=jnp.float32
    )
    flat_products = products.reshape(block_slots, BLOCK * ens_width)
    block_rows = jnp.where(live_mask, receptor_ids, window_blocks)
    evolved = lax.psum_scatter(
        grouped_sum(
            flat_products, block_rows, jnp.int32(0), own_blocks * lax.axis_size("region")
        ).astype(jnp.bfloat16),
        "region",
        scatter_dimension=0,
        tiled=True,
    ).astype(jnp.float32)
    difference = evolved.reshape(own_blocks * BLOCK, ens_width) - observed[0].astype(jnp.float32)
    misfit = (inv_var[0][:, None] * difference).astype(jnp.bfloat16)
    everything = lax.all_gather(
        misfit.reshape(own_blocks, BLOCK, ens_width), "region", axis=0, tiled=True
    )
    block_misfit = pick_rows(everything, receptor_ids)
    adjoints = jnp.einsum(
        "kab,kae->kbe", footprint, block_misfit, preferred_element_type=jnp.float32
    )
    panel_total = slice_total * cell_blocks
    panel_rows = jnp.where(live_mask, panel_ids, panel_total)
    collected = grouped_sum(
        adjoints.reshape(block_slots, BLOCK * ens_width), panel_rows, 0, panel_total
    )
    collected = collected.reshape(slice_total, cells_here, ens_width)
    weights = blend
    pulled = lax.psum_scatter(
        jnp.einsum("ts,tce->sce", weights, collected, precision=highest).astype(jnp.bfloat16),
        "window",
        scatter_dimension=0,
        tiled=True,
    )
    gradient = jnp.dot(
        pulled.reshape(slab_count * cells_here, ens_width),
        prior_mix,
        preferred_element_type=jnp.float32,
    )
    gradient = gradient.astype(jnp.bfloat16).reshape(slab_count, cells_here, ens_width)
    return (misfit.reshape(1, own_blocks * BLOCK, ens_width), gradient)


def solution(mesh):
    in_specs = (
        P(("group", "window"), "region", None),
        P(),
        P(("group", "window"), "region", None),
        P(("group", "window"), "region"),
        P(("group", "window"), "region"),
        P(("group", "window"), "region"),
        P(("group", "window"), "region"),
        P(("group", "window"), "region", None),
        P(("group", "window"), "region"),
        P(),
    )
    out_specs = (P(("group", "window"), "region", None), P(("group", "window"), "region", None))
    return jax.shard_map(shards, mesh=mesh, in_specs=in_specs, out_specs=out_specs, check_vma=False)
```

profile of v0, /device:TPU:0, one launch (start us, length us, event | category | flops | bytes accessed | tf_op | source)
XLA Modules:
  0.0 413.2 jit_solution(11258094702438953982)
XLA Ops:
  7.2 0.0 all-gather.2.cloned.1.call-start
  7.2 2.9 copy.24
  10.1 0.0 all-reduce.3.cloned.1.call-start
  10.8 12.0 %copy.27 = bf16[1,1024,4096]{1,2,0:T(8,128)(2,1)} copy(bf16[1,1024,4096]{2,1,0:T(8,128)(2,1)} %param.12) | data formatting | bytes 16777216 | tf_op args[2]
  22.9 29.3 %copy.32 = bf16[1024,64,64]{1,2,0:T(8,128)(2,1)} copy(bf16[1024,64,64]{0,2,1:T(8,128)(2,1)} %bitcast.78) | data formatting | bytes 16777216 | tf_op jit(solution)/shard_map/reshape;squeeze | solution.py:54
  52.2 3.4 convolution_convert_fusion.3
  55.6 0.5 copy.25
  56.2 8.5 %convolution_convert_fusion = bf16[1024,64,128]{2,0,1:T(8,128)(2,1)} fusion(bf16[128,64,128]{2,1,0:T(8,128)(2,1)S(1)} %bitcast.79, s32[1024]{0:T(1024)S(1)} %bitcast.85), kind=kOutput, calls=%fused_computation.14 | convolution fusion | flops 2156003328 | bytes 18878464 | tf_op jit(solution)/shard_map/kp,pbe->kbe/dot_general | solution.py:21
  64.7 32.5 %fusion.8 = f32[1024,128,64]{1,2,0:T(8,128)} fusion(bf16[1024,64,64]{1,2,0:T(8,128)(2,1)} %copy.32, bf16[1024,64,128]{2,0,1:T(8,128)(2,1)} %convolution_convert_fusion), kind=kOutput, calls=%fused_computation.11 | convolution fusion | flops 1073741824 | bytes 58720256 | tf_op jit(solution)/shard_map/kab,kbe->kae/dot_general | solution.py:58
  97.1 32.7 %fusion.2 = f32[16,8192]{1,0:T(8,128)S(1)} fusion(f32[128,8,64,128]{3,2,1,0:T(8,128)} %bitcast.74, s32[1024]{0:T(1024)S(1)} %fusion.42), kind=kOutput, calls=%fused_computation.6 | convolution fusion | flops 268451840 | bytes 34082816 | tf_op jit(solution)/shard_map/kl,kd->ld/dot_general | solution.py:14
  129.9 33.4 %fusion.18 = bf16[16,8192]{1,0:T(8,128)(2,1)} fusion(f32[16,8192]{1,0:T(8,128)S(1)} %fusion.2, f32[128,8,64,128]{3,2,1,0:T(8,128)} %bitcast.75, s32[1024]{0:T(1024)S(1)} %fusion.42), kind=kOutput, calls=%fused_computation.18 | convolution fusion | flops 302268416 | bytes 34344960 | tf_op jit(solution)/shard_map/kl,kd->ld/dot_general | solution.py:15
  163.3 0.0 reduce-scatter.4.cloned.1.call-start
  163.4 0.6 broadcast.33
  164.0 0.7 reduce.3
  164.7 0.1 mul.34
  164.8 0.7 dynamic-slice
  166.2 70.5 %all-reduce.3.cloned.1.call-done = bf16[16,8192]{1,0:T(8,128)(2,1)} async-done(((bf16[16,8192]{1,0:T(8,128)(2,1)}), bf16[16,8192]{1,0:T(8,128)(2,1)}) %all-reduce.3.cloned.1.call-update) | async-done | bytes 262160
  236.7 0.9 fusion.43
  237.7 0.1 fusion.35
  237.7 30.8 %all_gather.7 = bf16[16,64,128]{2,1,0:T(8,128)(2,1)S(1)} all-gather(bf16[2,64,128]{2,1,0:T(8,128)(2,1)S(1)} %fusion.35), channel_id=1, replica_groups=mesh['group'=2,'region'=8,'window'=2] {'region'}, dimensions={0}, use_global_device_ids=true | all-gather | bytes 294912 | tf_op jit(solution)/shard_map/all_gather | solution.py:73
  268.6 8.1 %convolution_convert_fusion.1 = bf16[1024,64,128]{2,0,1:T(8,128)(2,1)} fusion(bf16[16,64,128]{2,1,0:T(8,128)(2,1)S(1)} %all_gather.7, s32[1024]{0:T(1024)S(1)} %bitcast.88), kind=kOutput, calls=%fused_computation.15 | convolution fusion | flops 276840448 | bytes 17043456 | tf_op jit(solution)/shard_map/kp,pbe->kbe/dot_general | solution.py:21
  276.7 33.3 %fusion.6 = f32[1024,128,64]{1,2,0:T(8,128)} fusion(bf16[1024,64,64]{1,2,0:T(8,128)(2,1)} %copy.32, bf16[1024,64,128]{2,0,1:T(8,128)(2,1)} %convolution_convert_fusion.1), kind=kOutput, calls=%fused_computation.9 | convolution fusion | flops 1073741824 | bytes 58720256 | tf_op jit(solution)/shard_map/kab,kae->kbe/dot_general | solution.py:77
  310.0 31.7 %fusion.3 = f32[128,8192]{1,0:T(8,128)} fusion(f32[128,8,64,128]{3,2,1,0:T(8,128)} %bitcast.76, s32[1024]{0:T(1024)S(1)} %fusion.41), kind=kOutput, calls=%fused_computation.7 | convolution fusion | flops 2147614720 | bytes 37752832 | tf_op jit(solution)/shard_map/kl,kd->ld/dot_general | solution.py:14
  341.7 38.2 %fusion.12 = f32[128,8192]{1,0:T(8,128)} fusion(f32[128,8192]{1,0:T(8,128)} %fusion.3, f32[128,8,64,128]{3,2,1,0:T(8,128)} %bitcast.77, s32[1024]{0:T(1024)S(1)} %fusion.41), kind=kOutput, calls=%fused_computation.16 | convolution fusion | flops 2182217728 | bytes 41947136 | tf_op jit(solution)/shard_map/kl,kd->ld/dot_general | solution.py:15
  379.9 4.9 %reshape.83 = f32[16,512,128]{2,1,0:T(8,128)} reshape(f32[128,8192]{1,0:T(8,128)} %fusion.12) | data formatting | bytes 8388608 | tf_op jit(solution)/shard_map/reshape | solution.py:85
  384.8 8.2 %convert_bitcast_fusion = bf16[512,2,8,128]{3,2,1,0:T(8,128)(2,1)S(1)} fusion(f32[16,512,128]{2,1,0:T(8,128)} %reshape.83, f32[16,16]{1,0:T(8,128)S(1)} %copy-done.2), kind=kOutput, calls=%fused_computation.24 | convolution fusion | flops 202375168 | bytes 6292480 | tf_op jit(solution)/shard_map/ts,tce->sce/dot_general | solution.py:88
  393.0 1.5 copy.76
  394.5 0.1 reshape.80
  394.5 0.7 multiply_convert_fusion
  395.2 8.3 %reduce-scatter.4.cloned.1.call-done = bf16[8,65536]{1,0:T(8,128)(2,1)} async-done(((bf16[16,65536]{1,0:T(8,128)(2,1)}), bf16[8,65536]{1,0:T(8,128)(2,1)}) %reduce-scatter.4.cloned.1.call-update) | async-done | bytes 1048592
  403.5 1.4 copy.35
  404.9 1.4 convolution_convert_fusion.2
  (23 shorter events, 0.1 us)
Async XLA Ops:
  7.2 397.7 %copy-start = (bf16[128,128]{1,0:T(8,128)(2,1)S(1)}, bf16[128,128]{1,0:T(8,128)(2,1)}, u32[]{:S(2)}) copy-start(bf16[128,128]{1,0:T(8,128)(2,1)} %param.19) | copy-start | bytes 98308
  7.2 45.0 %all-gather.2.cloned.1.call-start = ((), (), s32[]{:S(2)}) async-start(), calls=%async_computation.1 | async-start | bytes 3145728 | tf_op jit(solution)/shard_map/all_gather | solution.py:50
  10.1 226.6 %all-reduce.3.cloned.1.call-start = ((), (), s32[]{:S(2)}) async-start(), calls=%async_computation.3 | async-start | bytes 524288
  22.9 29.3 %copy-start.3 = (s32[1,1024]{1,0:T(1,128)S(1)}, s32[1,1024]{1,0:T(1,128)}, u32[]{:S(2)}) copy-start(s32[1,1024]{1,0:T(1,128)} %param.13) | copy-start | bytes 12292
  22.9 29.3 %copy-start.4 = (s32[1,1024]{1,0:T(1,128)S(1)}, s32[1,1024]{1,0:T(1,128)}, u32[]{:S(2)}) copy-start(s32[1,1024]{1,0:T(1,128)} %param.14) | copy-start | bytes 12292
  22.9 29.3 %copy-start.5 = (s32[1,1024]{1,0:T(1,128)S(1)}, s32[1,1024]{1,0:T(1,128)}, u32[]{:S(2)}) copy-start(s32[1,1024]{1,0:T(1,128)} %param.15) | copy-start | bytes 12292
  22.9 29.3 %copy-start.2 = (f32[16,16]{1,0:T(8,128)S(1)}, f32[16,16]{1,0:T(8,128)}, u32[]{:S(2)}) copy-start(f32[16,16]{1,0:T(8,128)} %param.11) | copy-start | bytes 3076
  129.8 34.2 %copy-start.6 = (f32[1,128]{1,0:T(1,128)S(1)}, f32[1,128]{1,0:T(1,128)}, u32[]{:S(2)}) copy-start(f32[1,128]{1,0:T(1,128)} %param.18) | copy-start | bytes 1540
  129.8 34.9 %copy-start.7 = (u32[32]{0:T(128)S(1)}, u32[32]{0:T(128)}, u32[]{:S(2)}) copy-start(u32[32]{0:T(128)} %constant.15) | copy-start | bytes 388
  129.8 107.8 %copy-start.1 = (bf16[1,128,128]{2,1,0:T(8,128)(2,1)S(1)}, bf16[1,128,128]{2,1,0:T(8,128)(2,1)}, u32[]{:S(2)}) copy-start(bf16[1,128,128]{2,1,0:T(8,128)(2,1)} %param.17) | copy-start | bytes 98308
  163.3 240.2 %reduce-scatter.4.cloned.1.call-start = ((), (), s32[]{:S(2)}) async-start(), calls=%async_computation.2 | async-start | bytes 3145728
Sparse Core Ops, SparseCore 0:
  10.2 13.0 all-gather.1
  163.5 73.1 all-reduce.2
  394.6 8.8 reduce-scatter.3
where the time goes:
time: 420 us; the launch traced here: 413 us
  matrix products  231 us (55%)
  waiting for transfers between devices  78.9 us (19%)
  local copies, waits for them, and re-layouts  53.9 us (13%)
  blocking collectives  30.8 us (7%)
  between operations  15.7 us (4%)
    unnamed x5, waiting for transfers between devices  78.9 us
    dot_general x2, matrix products, grouped_sum(): jnp.einsum('kl,kd->ld', table, low_part, preferred_element_type=jnp.float32)  71.7 us
    dot_general x2, matrix products, grouped_sum(): jnp.einsum('kl,kd->ld', table, high_part, preferred_element_type=jnp.floa...  64.4 us
    dot_general x1, matrix products, shards(): jnp.einsum('kab,kae->kbe', footprint, block_misfit, preferred_element_typ...  33.3 us
    dot_general x1, matrix products, shards(): jnp.einsum('kab,kbe->kae', footprint, pick_rows(panels, panel_ids), prefe...  32.5 us
    all_gather x1, blocking collectives, shards(): lax.all_gather(misfit.reshape(own_blocks, BLOCK, ens_width), 'region', ax...  30.8 us
    another operation x1, local copies, waits for them, and re-layouts, shards(): footprint = footprints[0].reshape(block_slots, BLOCK, BLOCK)  29.3 us
    unnamed x21, local copies, waits for them, and re-layouts  17.7 us
  transfers between devices with their start and end apart: 3, of which 2 were waited for; matrix products, arithmetic and copies ran while one was open for 11% of the time, Pallas kernels for 0%

commit v1 on v0

v1 whole, which is shorter than its diff:
```python
import functools

import jax
import jax.numpy as jnp
from jax import lax
from jax.experimental import pallas as pl
from jax.experimental.pallas import tpu as pltpu
from jax.sharding import PartitionSpec as P

BLOCK = 64
MESH = pl.DeviceIdType.MESH
F32 = jnp.float32
BF16 = jnp.bfloat16
STEP = 128
SUB = 16
CELLS_AT_ONCE = 16
PIECES = 4


def spread(matrix, width):
    size = matrix.shape[0]
    full = size * width
    row = lax.broadcasted_iota(jnp.int32, (full, size), 0)
    col = lax.broadcasted_iota(jnp.int32, (full, size), 1)
    pick = (row // width == col).astype(BF16)
    row_f = lax.broadcasted_iota(jnp.int32, (full, full), 0)
    col_f = lax.broadcasted_iota(jnp.int32, (full, full), 1)
    same = row_f % width == col_f % width
    high = matrix.astype(BF16)
    low = (matrix - high.astype(F32)).astype(BF16)
    parts = []
    for part in (high, low):
        tall = jnp.dot(pick, part, preferred_element_type=F32).astype(BF16)
        wide = lax.dot_general(tall, pick, (((1,), (1,)), ((), ())), preferred_element_type=F32)
        parts.append(jnp.where(same, wide, 0.0).astype(BF16))
    return parts


def blend_kernel(blend_ref, flux_ref, panels_ref, full, local_sem, send_sem, recv_sem):
    me = lax.axis_index("window")
    other = 1 - me
    slabs, cells, ens = flux_ref.shape
    slices = panels_ref.shape[0]
    barrier = pltpu.get_barrier_semaphore()
    pl.semaphore_signal(barrier, inc=1, device_id={"window": other}, device_id_type=MESH)
    piece = cells // PIECES
    locals_, sends = [], []
    for k in range(PIECES):
        span = pl.ds(k * piece, piece)
        locals_.append(
            pltpu.make_async_copy(
                flux_ref.at[:, span, :], full.at[pl.ds(me * slabs, slabs), span, :], local_sem.at[k]
            )
        )
        locals_[-1].start()
    pl.semaphore_wait(barrier, 1)
    for k in range(PIECES):
        span = pl.ds(k * piece, piece)
        sends.append(
            pltpu.make_async_remote_copy(
                src_ref=flux_ref.at[:, span, :],
                dst_ref=full.at[pl.ds(me * slabs, slabs), span, :],
                send_sem=send_sem.at[k],
                recv_sem=recv_sem.at[k],
                device_id={"window": other},
                device_id_type=MESH,
            )
        )
        sends[-1].start()
    high, low = spread(blend_ref[...], CELLS_AT_ONCE)
    for k in range(PIECES):
        locals_[k].wait()
        sends[k].wait_recv()

        def group(g, carry, k=k):
            sides = []
            for half in range(2):
                start = pl.multiple_of(k * piece + g * 2 * CELLS_AT_ONCE + half * CELLS_AT_ONCE, CELLS_AT_ONCE)
                sides.append(full[:, pl.ds(start, CELLS_AT_ONCE), :].reshape(slices * CELLS_AT_ONCE, ens))
            rhs = jnp.concatenate(sides, axis=1)
            out = jnp.dot(high, rhs, preferred_element_type=F32) + jnp.dot(low, rhs, preferred_element_type=F32)
            out = out.astype(BF16)
            for half in range(2):
                start = pl.multiple_of(k * piece + g * 2 * CELLS_AT_ONCE + half * CELLS_AT_ONCE, CELLS_AT_ONCE)
                panels_ref[:, pl.ds(start, CELLS_AT_ONCE), :] = out[:, half * ens : (half + 1) * ens].reshape(
                    slices, CELLS_AT_ONCE, ens
                )
            return carry

        lax.fori_loop(0, piece // (2 * CELLS_AT_ONCE), group, 0, unroll=2)
    for k in range(PIECES):
        sends[k].wait_send()


def split_rows(f):
    lower = lax.broadcasted_iota(jnp.int32, f.shape, 1) < BLOCK
    zero = jnp.zeros_like(f)
    return jnp.concatenate([jnp.where(lower, f, zero), jnp.where(lower, zero, f)], axis=0)


def forward_kernel(to_ref, from_ref, fp_ref, panels_ref, frel_ref, part_ref, acc):
    step = pl.program_id(0)
    count = part_ref.shape[0]

    @pl.when(step == 0)
    def _():
        acc[...] = jnp.zeros_like(acc)

    def body(g, carry):
        base = pl.multiple_of(g * SUB, SUB)
        x = fp_ref[pl.ds(base, SUB), :].reshape(SUB, BLOCK // 2, 2 * BLOCK)
        frel_ref[pl.ds(base, SUB)] = x
        for j in range(SUB):
            slot = step * STEP + base + j
            p = panels_ref[from_ref[slot]]
            d = jnp.dot(split_rows(x[j]), jnp.concatenate([p, p], axis=0), preferred_element_type=F32)
            q = to_ref[slot]
            acc[q] += d
        return carry

    lax.fori_loop(0, STEP // SUB, body, 0)

    @pl.when(step == pl.num_programs(0) - 1)
    def _():
        part_ref[...] = acc[pl.ds(0, count)].astype(BF16)


def exchange_kernel(regions, part_ref, obs_ref, inv_ref, all_ref, own_ref, got, send_a, recv_a, send_b, recv_b):
    me = lax.axis_index("region")
    rows, ens = obs_ref.shape
    barrier = pltpu.get_barrier_semaphore()
    for k in range(1, regions):
        peer = lax.rem(me + k, regions)
        pl.semaphore_signal(barrier, inc=1, device_id={"region": peer}, device_id_type=MESH)
    row = lax.broadcasted_iota(jnp.int32, (rows, rows), 0)
    col = lax.broadcasted_iota(jnp.int32, (rows, rows), 1)
    inner = row % BLOCK
    half = BLOCK // 2
    picked = (row // BLOCK) * BLOCK + (inner % half) * 2 + inner // half == col
    table = picked.astype(BF16)
    obs = jnp.dot(table, obs_ref[...], preferred_element_type=F32)
    inv = jnp.sum(jnp.where(picked, inv_ref[...], 0.0), axis=1, keepdims=True)
    pl.semaphore_wait(barrier, regions - 1)

    def first(k):
        peer = lax.rem(me + k, regions)
        return pltpu.make_async_remote_copy(
            src_ref=part_ref.at[peer],
            dst_ref=got.at[k],
            send_sem=send_a.at[k],
            recv_sem=recv_a.at[k],
            device_id={"region": peer},
            device_id_type=MESH,
        )

    def second(k):
        peer = lax.rem(me + k, regions)
        return pltpu.make_async_remote_copy(
            src_ref=all_ref.at[me],
            dst_ref=all_ref.at[me],
            send_sem=send_b.at[k],
            recv_sem=recv_b.at[k],
            device_id={"region": peer},
            device_id_type=MESH,
        )

    firsts = [first(k) for k in range(1, regions)]
    for copy in firsts:
        copy.start()
    evolved = part_ref[me].astype(F32)
    for k in range(1, regions):
        firsts[k - 1].wait_recv()
        evolved = evolved + got[k].astype(F32)
    misfit = (inv * (evolved - obs)).astype(BF16)
    all_ref[me] = misfit
    seconds = [second(k) for k in range(1, regions)]
    for copy in seconds:
        copy.start()
    own_ref[...] = lax.dot_general(
        table, misfit, (((0,), (0,)), ((), ())), preferred_element_type=F32
    ).astype(BF16)
    for copy in firsts:
        copy.wait_send()
    for k in range(1, regions):
        source = lax.rem(me - k + regions, regions)
        pltpu.make_async_remote_copy(
            src_ref=all_ref.at[source],
            dst_ref=all_ref.at[source],
            send_sem=send_b.at[k],
            recv_sem=recv_b.at[k],
            device_id={"region": source},
            device_id_type=MESH,
        ).wait_recv()
    for copy in seconds:
        copy.wait_send()


def adjoint_kernel(to_ref, from_ref, blend_ref, frel_ref, misfit_ref, pulled_ref, acc):
    step = pl.program_id(0)
    slices, cells, ens = pulled_ref.shape

    @pl.when(step == 0)
    def _():
        acc[...] = jnp.zeros_like(acc)

    def body(g, carry):
        base = pl.multiple_of(g * SUB, SUB)
        for j in range(SUB):
            slot = step * STEP + base + j
            m = misfit_ref[from_ref[slot]]
            d = lax.dot_general(
                split_rows(frel_ref[base + j]), m, (((0,), (0,)), ((), ())), preferred_element_type=F32
            )
            p = to_ref[slot]
            acc[p] += d[:BLOCK] + d[BLOCK:]
        return carry

    lax.fori_loop(0, STEP // SUB, body, 0)

    @pl.when(step == pl.num_programs(0) - 1)
    def _():
        high, low = spread(blend_ref[...], CELLS_AT_ONCE)
        blocks = cells // BLOCK
        shape = (slices * CELLS_AT_ONCE, ens)

        def group(g, carry):
            block = g // (BLOCK // (2 * CELLS_AT_ONCE))
            within = g % (BLOCK // (2 * CELLS_AT_ONCE))
            sides = []
            for half in range(2):
                start = pl.multiple_of(within * 2 * CELLS_AT_ONCE + half * CELLS_AT_ONCE, CELLS_AT_ONCE)
                rows = [acc[t * blocks + block, pl.ds(start, CELLS_AT_ONCE), :] for t in range(slices)]
                sides.append(jnp.concatenate(rows, axis=0))
            rhs = jnp.concatenate(sides, axis=1)
            rhs_high = rhs.astype(BF16)
            rhs_low = (rhs - rhs_high.astype(F32)).astype(BF16)
            dims = (((0,), (0,)), ((), ()))
            out = lax.dot_general(high, rhs_high, dims, preferred_element_type=F32)
            out = out + lax.dot_general(low, rhs_high, dims, preferred_element_type=F32)
            out = (out + lax.dot_general(high, rhs_low, dims, preferred_element_type=F32)).astype(BF16)
            for half in range(2):
                start = pl.multiple_of((g * 2 + half) * CELLS_AT_ONCE, CELLS_AT_ONCE)
                pulled_ref[:, pl.ds(start, CELLS_AT_ONCE), :] = out[:, half * ens : (half + 1) * ens].reshape(
                    slices, CELLS_AT_ONCE, ens
                )
            return carry

        lax.fori_loop(0, cells // (2 * CELLS_AT_ONCE), group, 0)


def gradient_kernel(pulled_ref, mix_ref, grad_ref, got, send_sem, recv_sem):
    me = lax.axis_index("window")
    other = 1 - me
    slabs, cells, ens = grad_ref.shape
    barrier = pltpu.get_barrier_semaphore()
    pl.semaphore_signal(barrier, inc=1, device_id={"window": other}, device_id_type=MESH)
    pl.semaphore_wait(barrier, 1)
    sends = []
    for k in range(slabs):
        sends.append(
            pltpu.make_async_remote_copy(
                src_ref=pulled_ref.at[other * slabs + k],
                dst_ref=got.at[k],
                send_sem=send_sem.at[k],
                recv_sem=recv_sem.at[k],
                device_id={"window": other},
                device_id_type=MESH,
            )
        )
        sends[-1].start()
    mix = mix_ref[...]
    for k in range(slabs):
        sends[k].wait_recv()
        total = (pulled_ref[me * slabs + k].astype(F32) + got[k].astype(F32)).astype(BF16)
        grad_ref[k] = jnp.dot(total, mix, preferred_element_type=F32).astype(BF16)
    for k in range(slabs):
        sends[k].wait_send()


def vmem():
    return pl.BlockSpec(memory_space=pltpu.VMEM)


def shards(
    regions,
    flux,
    blend,
    footprints,
    receptor_block,
    cell_block,
    slice_index,
    live_counts,
    observed,
    inv_var,
    prior_mix,
):
    slabs, cells, ens = flux.shape
    slices = blend.shape[0]
    cell_blocks = cells // BLOCK
    panel_total = slices * cell_blocks
    slots = footprints.shape[1]
    rows = observed.shape[1]
    own_blocks = rows // BLOCK
    window_blocks = own_blocks * regions

    live = jnp.arange(slots) < live_counts[0, 0]
    panel_ids = slice_index[0] * cell_blocks + cell_block[0]
    receptor_to = jnp.where(live, receptor_block[0], window_blocks)
    receptor_from = jnp.where(live, receptor_block[0], 0)
    panel_to = jnp.where(live, panel_ids, panel_total)
    panel_from = jnp.where(live, panel_ids, 0)

    panels = pl.pallas_call(
        blend_kernel,
        out_shape=jax.ShapeDtypeStruct((slices, cells, ens), BF16),
        in_specs=[vmem(), pl.BlockSpec(memory_space=pl.ANY)],
        out_specs=vmem(),
        scratch_shapes=[
            pltpu.VMEM((slices, cells, ens), BF16),
            pltpu.SemaphoreType.DMA((PIECES,)),
            pltpu.SemaphoreType.DMA((PIECES,)),
            pltpu.SemaphoreType.DMA((PIECES,)),
        ],
        compiler_params=pltpu.CompilerParams(collective_id=0, has_side_effects=True, vmem_limit_bytes=32 << 20),
        name="blend_slices",
    )(blend, flux)

    frel, part = pl.pallas_call(
        forward_kernel,
        out_shape=(
            jax.ShapeDtypeStruct((slots, BLOCK // 2, 2 * BLOCK), BF16),
            jax.ShapeDtypeStruct((window_blocks, BLOCK, ens), BF16),
        ),
        grid_spec=pltpu.PrefetchScalarGridSpec(
            num_scalar_prefetch=2,
            grid=(slots // STEP,),
            in_specs=[
                pl.BlockSpec((STEP, BLOCK * BLOCK), lambda i, a, b: (i, 0)),
                pl.BlockSpec((panel_total, BLOCK, ens), lambda i, a, b: (0, 0, 0)),
            ],
            out_specs=[
                pl.BlockSpec((STEP, BLOCK // 2, 2 * BLOCK), lambda i, a, b: (i, 0, 0)),
                pl.BlockSpec((window_blocks, BLOCK, ens), lambda i, a, b: (0, 0, 0)),
            ],
            scratch_shapes=[pltpu.VMEM((window_blocks + 1, BLOCK, ens), F32)],
        ),
        compiler_params=pltpu.CompilerParams(vmem_limit_bytes=32 << 20),
        name="forward_blocks",
    )(receptor_to, panel_from, footprints[0], panels.reshape(panel_total, BLOCK, ens))

    misfit_all, misfit = pl.pallas_call(
        functools.partial(exchange_kernel, regions),
        out_shape=(
            jax.ShapeDtypeStruct((regions, rows, ens), BF16),
            jax.ShapeDtypeStruct((rows, ens), BF16),
        ),
        in_specs=[vmem()] * 3,
        out_specs=(vmem(), vmem()),
        scratch_shapes=[
            pltpu.VMEM((regions, rows, ens), BF16),
            pltpu.SemaphoreType.DMA((regions,)),
            pltpu.SemaphoreType.DMA((regions,)),
            pltpu.SemaphoreType.DMA((regions,)),
            pltpu.SemaphoreType.DMA((regions,)),
        ],
        compiler_params=pltpu.CompilerParams(collective_id=1, has_side_effects=True, vmem_limit_bytes=32 << 20),
        name="misfit_exchange",
    )(part.reshape(regions, rows, ens), observed[0], inv_var)

    pulled = pl.pallas_call(
        adjoint_kernel,
        out_shape=jax.ShapeDtypeStruct((slices, cells, ens), BF16),
        grid_spec=pltpu.PrefetchScalarGridSpec(
            num_scalar_prefetch=2,
            grid=(slots // STEP,),
            in_specs=[
                pl.BlockSpec((slices, slices), lambda i, a, b: (0, 0)),
                pl.BlockSpec((STEP, BLOCK // 2, 2 * BLOCK), lambda i, a, b: (i, 0, 0)),
                pl.BlockSpec((window_blocks, BLOCK, ens), lambda i, a, b: (0, 0, 0)),
            ],
            out_specs=pl.BlockSpec((slices, cells, ens), lambda i, a, b: (0, 0, 0)),
            scratch_shapes=[pltpu.VMEM((panel_total + 1, BLOCK, ens), F32)],
        ),
        compiler_params=pltpu.CompilerParams(vmem_limit_bytes=32 << 20),
        name="adjoint_blocks",
    )(panel_to, receptor_from, blend, frel, misfit_all.reshape(window_blocks, BLOCK, ens))

    gradient = pl.pallas_call(
        gradient_kernel,
        out_shape=jax.ShapeDtypeStruct((slabs, cells, ens), BF16),
        in_specs=[vmem(), vmem()],
        out_specs=vmem(),
        scratch_shapes=[
            pltpu.VMEM((slabs, cells, ens), BF16),
            pltpu.SemaphoreType.DMA((slabs,)),
            pltpu.SemaphoreType.DMA((slabs,)),
        ],
        compiler_params=pltpu.CompilerParams(collective_id=2, has_side_effects=True, vmem_limit_bytes=32 << 20),
        name="gradient_exchange",
    )(pulled, prior_mix)
    return misfit[None], gradient


def solution(mesh):
    in_specs = (
        P(("group", "window"), "region", None),
        P(),
        P(("group", "window"), "region", None),
        P(("group", "window"), "region"),
        P(("group", "window"), "region"),
        P(("group", "window"), "region"),
        P(("group", "window"), "region"),
        P(("group", "window"), "region", None),
        P(("group", "window"), "region"),
        P(),
    )
    out_specs = (P(("group", "window"), "region", None), P(("group", "window"), "region", None))
    return jax.shard_map(
        functools.partial(shards, mesh.shape["region"]),
        mesh=mesh,
        in_specs=in_specs,
        out_specs=out_specs,
        check_vma=False,
    )
```

time: 420 us -> 83.7 us (0.20); the launches traced: 413 us -> 83.2 us
  matrix products: 231 us -> 0 us
  waiting for transfers between devices: 78.9 us -> 0 us
  Pallas kernels: 0 us -> 73.5 us
  local copies, waits for them, and re-layouts: 53.9 us -> 6.9 us
  blocking collectives: 30.8 us -> 0 us
  between operations: 15.7 us -> 1.4 us
    dot_general x11 -> x0, matrix products: 231 us -> none  [the longest x2 71.7 us: grouped_sum(): jnp.einsum('kl,kd->ld', table, low_part, preferred_element_type=jnp.float32)]
    unnamed x5 -> x0, waiting for transfers between devices: 78.9 us -> none
    pallas_call x0 -> x5, Pallas kernels: none -> 73.5 us  [the longest x1 28.6 us: shards(): pl.pallas_call(adjoint_kernel, out_shape=jax.ShapeDtypeStruct((slices, ce...]
    all_gather x1 -> x0, blocking collectives: 30.8 us -> none  [shards(): lax.all_gather(misfit.reshape(own_blocks, BLOCK, ens_width), 'region', ax...]
    another operation x1 -> x0, local copies, waits for them, and re-layouts: 29.3 us -> none  [shards(): footprint = footprints[0].reshape(block_slots, BLOCK, BLOCK)]
    unnamed x21 -> x16, local copies, waits for them, and re-layouts: 17.7 us -> 6.9 us
    reshape x2 -> x0, local copies, waits for them, and re-layouts: 4.95 us -> none  [the longest x1 4.89 us: shards(): collected = collected.reshape(slice_total, cells_here, ens_width)]
  transfers between devices with their start and end apart: 3 -> 0, of which waited for: 2 -> 0; matrix products, arithmetic and copies ran while one was open for 11% -> 0% of each run, Pallas kernels for 0% -> 0%
where the time goes in v1:
time: 83.7 us; the launch traced here: 83.2 us
  Pallas kernels  73.5 us (88%)
  local copies, waits for them, and re-layouts  6.9 us (8%)
  other arithmetic  1.4 us (2%)
  between operations  1.4 us (2%)
    pallas_call x1, Pallas kernels, shards(): pl.pallas_call(adjoint_kernel, out_shape=jax.ShapeDtypeStruct((slices, ce...  28.6 us
    pallas_call x1, Pallas kernels, shards(): pl.pallas_call(forward_kernel, out_shape=(jax.ShapeDtypeStruct((slots, BL...  18.8 us
    pallas_call x1, Pallas kernels, shards(): pl.pallas_call(functools.partial(exchange_kernel, regions), out_shape=(ja...  18.6 us
    unnamed x16, local copies, waits for them, and re-layouts  6.9 us
    pallas_call x1, Pallas kernels, shards(): pl.pallas_call(blend_kernel, out_shape=jax.ShapeDtypeStruct((slices, cell...  4.28 us
    pallas_call x1, Pallas kernels, shards(): pl.pallas_call(gradient_kernel, out_shape=jax.ShapeDtypeStruct((slabs, ce...  3.14 us

profile of v1, /device:TPU:0, one launch (start us, length us, event | category | flops | bytes accessed | tf_op | source)
XLA Modules:
  0.0 83.2 jit_solution(13434846009401120007)
XLA Ops:
  0.6 0.0 copy-start.5
  0.6 0.0 copy-start.6
  0.7 0.0 copy-start.3
  1.3 0.7 multiply_add_fusion
  2.0 0.7 fusion
  2.7 0.0 copy-start.1
  2.7 1.2 %copy-done.1 = bf16[8,512,128]{2,1,0:T(8,128)(2,1)S(1)} copy-done((bf16[8,512,128]{2,1,0:T(8,128)(2,1)S(1)}, bf16[8,512,128]{2,1,0:T(8,128)(2,1)}, u32[]{:S(2)}) %copy-start.1) | copy-done | bytes 1048600
  4.0 0.0 copy-start.4
  4.0 0.7 copy-done.4
  4.6 4.3 %blend_slices.1 = bf16[16,512,128]{2,1,0:T(8,128)(2,1)S(1)} custom-call(f32[16,16]{1,0:T(8,128)S(1)} %copy-done.4, bf16[8,512,128]{2,1,0:T(8,128)(2,1)S(1)} %copy-done.1), custom_call_target="tpu_custom_call" | custom-call | tf_op jit(solution)/shard_map/blend_slices/pallas_call | solution.py:313
  8.9 0.0 copy-start
  8.9 3.4 %copy-done = bf16[1,1024,4096]{2,1,0:T(8,128)(2,1)S(1)} copy-done((bf16[1,1024,4096]{2,1,0:T(8,128)(2,1)S(1)}, bf16[1,1024,4096]{2,1,0:T(8,128)(2,1)}, u32[]{:S(2)}) %copy-start) | copy-done | bytes 8388632
  12.3 0.0 copy-start.2
  12.3 18.8 %forward_blocks.1 = (bf16[1024,32,128]{2,1,0:T(8,128)(2,1)S(1)}, bf16[16,64,128]{2,1,0:T(8,128)(2,1)S(1)}) custom-call(s32[1024]{0:T(1024)S(1)} %get-tuple-element.11.to_ref, s32[1024]{0:T(1024)S(1)} %get-tuple-element.14.from_ref, bf16[1024,4096]{1,0:T(8,128)(2,1)S(1)} %bitcast.10, bf16[128,64,128]{2,1,0:T(8,128)(2,1)S(1)} %bitcast.11), custom_call_target="tpu_custom_call" | custom-call | tf_op jit(solution)/shard_map/forward_blocks/pallas_call | solution.py:328
  31.2 0.0 copy-done.6
  31.2 0.0 copy-done.3
  31.2 18.6 %misfit_exchange.1 = (bf16[8,128,128]{2,1,0:T(8,128)(2,1)S(1)}, bf16[128,128]{1,0:T(8,128)(2,1)S(1)}) custom-call(bf16[8,128,128]{2,1,0:T(8,128)(2,1)S(1)} %bitcast.12, bf16[128,128]{1,0:T(8,128)(2,1)S(1)} %bitcast.14, f32[1,128]{1,0:T(1,128)S(1)} %copy-done.6), custom_call_target="tpu_custom_call" | custom-call | tf_op jit(solution)/shard_map/misfit_exchange/pallas_call | solution.py:351
  49.8 0.0 copy-done.5
  49.8 28.6 %adjoint_blocks.1.pulled_ref = bf16[16,512,128]{2,1,0:T(8,128)(2,1)S(1)} custom-call(s32[1024]{0:T(1024)S(1)} %get-tuple-element.15.to_ref, s32[1024]{0:T(1024)S(1)} %get-tuple-element.10.from_ref, f32[16,16]{1,0:T(8,128)S(1)} %copy-done.5, bf16[1024,32,128]{2,1,0:T(8,128)(2,1)S(1)} %get-tuple-element.8.frel_ref, bf16[16,64,128]{2,1,0:T(8,128)(2,1)S(1)} %bitcast.13), custom_call_target="tpu_custom_call" | custom-call | tf_op jit(solution)/shard_map/adjoint_blocks/pallas_call | solution.py:370
  78.4 0.0 copy-done.2
  78.4 3.1 %gradient_exchange.1 = bf16[8,512,128]{2,1,0:T(8,128)(2,1)S(1)} custom-call(bf16[16,512,128]{2,1,0:T(8,128)(2,1)S(1)} %adjoint_blocks.1.pulled_ref, bf16[128,128]{1,0:T(8,128)(2,1)S(1)} %copy-done.2), custom_call_target="tpu_custom_call" | custom-call | tf_op jit(solution)/shard_map/gradient_exchange/pallas_call | solution.py:388
  81.6 0.6 copy.15
  82.2 1.0 %copy.16 = bf16[8,512,128]{2,1,0:T(8,128)(2,1)} copy(bf16[8,512,128]{2,1,0:T(8,128)(2,1)S(1)} %gradient_exchange.1) | data formatting | bytes 2097152
Async XLA Ops:
  0.6 49.2 %copy-start.5 = (f32[16,16]{1,0:T(8,128)S(1)}, f32[16,16]{1,0:T(8,128)}, u32[]{:S(2)}) copy-start(f32[16,16]{1,0:T(8,128)} %blend_ref.3) | copy-start | bytes 3076
  0.6 30.5 %copy-start.6 = (f32[1,128]{1,0:T(1,128)S(1)}, f32[1,128]{1,0:T(1,128)}, u32[]{:S(2)}) copy-start(f32[1,128]{1,0:T(1,128)} %inv_ref.1) | copy-start | bytes 1540
  0.7 30.5 %copy-start.3 = (bf16[1,128,128]{2,1,0:T(8,128)(2,1)S(1)}, bf16[1,128,128]{2,1,0:T(8,128)(2,1)}, u32[]{:S(2)}) copy-start(bf16[1,128,128]{2,1,0:T(8,128)(2,1)} %param.17) | copy-start | bytes 98308
  2.7 1.2 %copy-start.1 = (bf16[8,512,128]{2,1,0:T(8,128)(2,1)S(1)}, bf16[8,512,128]{2,1,0:T(8,128)(2,1)}, u32[]{:S(2)}) copy-start(bf16[8,512,128]{2,1,0:T(8,128)(2,1)} %flux_ref.1) | copy-start | bytes 3145732
  4.0 0.7 copy-start.4
  8.9 3.4 %copy-start = (bf16[1,1024,4096]{2,1,0:T(8,128)(2,1)S(1)}, bf16[1,1024,4096]{2,1,0:T(8,128)(2,1)}, u32[]{:S(2)}) copy-start(bf16[1,1024,4096]{2,1,0:T(8,128)(2,1)} %param.12) | copy-start | bytes 25165828
  12.3 66.1 %copy-start.2 = (bf16[128,128]{1,0:T(8,128)(2,1)S(1)}, bf16[128,128]{1,0:T(8,128)(2,1)}, u32[]{:S(2)}) copy-start(bf16[128,128]{1,0:T(8,128)(2,1)} %mix_ref.1) | copy-start | bytes 98308

commit v2 on v1

v2 whole, which is shorter than its diff:
```python
import functools

import jax
import jax.numpy as jnp
from jax import lax
from jax.experimental import pallas as pl
from jax.experimental.pallas import tpu as pltpu
from jax.sharding import PartitionSpec as P

BLOCK = 64
MESH = pl.DeviceIdType.MESH
F32 = jnp.float32
BF16 = jnp.bfloat16
SUB = 16
CELLS_AT_ONCE = 16
PIECES = 4
LOADS = 8
PAIRS = 8
TURNS = 8
LAG = 2


def spread(matrix, width):
    size = matrix.shape[0]
    full = size * width
    row = lax.broadcasted_iota(jnp.int32, (full, size), 0)
    col = lax.broadcasted_iota(jnp.int32, (full, size), 1)
    pick = (row // width == col).astype(BF16)
    row_f = lax.broadcasted_iota(jnp.int32, (full, full), 0)
    col_f = lax.broadcasted_iota(jnp.int32, (full, full), 1)
    same = row_f % width == col_f % width
    high = matrix.astype(BF16)
    low = (matrix - high.astype(F32)).astype(BF16)
    parts = []
    for part in (high, low):
        tall = jnp.dot(pick, part, preferred_element_type=F32).astype(BF16)
        wide = lax.dot_general(tall, pick, (((1,), (1,)), ((), ())), preferred_element_type=F32)
        parts.append(jnp.where(same, wide, 0.0).astype(BF16))
    return parts


def halves_swapped(x):
    return pltpu.roll(x, BLOCK, 1)


def blend_kernel(
    window_blocks,
    recv_ref,
    cell_ref,
    slice_ref,
    live_ref,
    blend_hbm,
    flux_hbm,
    fp_hbm,
    panels_ref,
    pairs_ref,
    index_ref,
    full,
    raw,
    blend_ref,
    blend_sem,
    fp_sem,
    local_sem,
    send_sem,
    recv_sem,
):
    me = lax.axis_index("window")
    other = 1 - me
    slabs, cells, ens = flux_hbm.shape
    slices = panels_ref.shape[0]
    slots = raw.shape[0]
    barrier = pltpu.get_barrier_semaphore()
    pl.semaphore_signal(barrier, inc=1, device_id={"window": other}, device_id_type=MESH)
    blend_copy = pltpu.make_async_copy(blend_hbm, blend_ref, blend_sem)
    blend_copy.start()
    piece = cells // PIECES
    locals_, sends, loads = [], [], []
    for k in range(PIECES):
        span = pl.ds(k * piece, piece)
        locals_.append(
            pltpu.make_async_copy(
                flux_hbm.at[:, span, :], full.at[pl.ds(me * slabs, slabs), span, :], local_sem.at[k]
            )
        )
        locals_[-1].start()
    part = slots // LOADS
    for k in range(LOADS):
        span = pl.ds(k * part, part)
        loads.append(pltpu.make_async_copy(fp_hbm.at[0, span, :], raw.at[span, :], fp_sem.at[k]))
    loads[0].start()
    pl.semaphore_wait(barrier, 1)
    for k in range(PIECES):
        span = pl.ds(k * piece, piece)
        sends.append(
            pltpu.make_async_remote_copy(
                src_ref=flux_hbm.at[:, span, :],
                dst_ref=full.at[pl.ds(me * slabs, slabs), span, :],
                send_sem=send_sem.at[k],
                recv_sem=recv_sem.at[k],
                device_id={"window": other},
                device_id_type=MESH,
            )
        )
        sends[-1].start()
    for k in range(1, LOADS):
        loads[k].start()

    cell_blocks = cells // BLOCK
    live = lax.broadcasted_iota(jnp.int32, recv_ref.shape, 1) < live_ref[...]
    panel = slice_ref[...] * cell_blocks + cell_ref[...]
    index_ref[pl.ds(0, 1), :] = jnp.where(live, recv_ref[...], window_blocks)
    index_ref[pl.ds(1, 1), :] = jnp.where(live, panel, 0)
    index_ref[pl.ds(2, 1), :] = jnp.where(live, panel, slices * cell_blocks)
    index_ref[pl.ds(3, 1), :] = jnp.where(live, recv_ref[...], 0)
    blend_copy.wait()
    high, low = spread(blend_ref[...], CELLS_AT_ONCE)

    def arrange(k):
        loads[k].wait()

        def body(g, carry):
            base = pl.multiple_of(k * part + g * SUB, SUB)
            x = raw[pl.ds(base, SUB), :].reshape(SUB, BLOCK // 2, 2 * BLOCK)
            lower = lax.broadcasted_iota(jnp.int32, (BLOCK // 2, 2 * BLOCK), 1) < BLOCK
            for j in range(0, SUB, 2):
                one, two = x[j], x[j + 1]
                even = jnp.where(lower, one, halves_swapped(two))
                odd = jnp.where(lower, halves_swapped(one), two)
                pairs_ref[k * (part // 2) + g * (SUB // 2) + j // 2] = jnp.concatenate([even, odd], axis=0)
            return carry

        lax.fori_loop(0, part // SUB, body, 0)

    for k in range(LOADS // 2):
        arrange(k)
    for k in range(PIECES):
        locals_[k].wait()
        sends[k].wait_recv()

        def group(g, carry, k=k):
            sides = []
            for half in range(2):
                start = pl.multiple_of(k * piece + g * 2 * CELLS_AT_ONCE + half * CELLS_AT_ONCE, CELLS_AT_ONCE)
                sides.append(full[:, pl.ds(start, CELLS_AT_ONCE), :].reshape(slices * CELLS_AT_ONCE, ens))
            rhs = jnp.concatenate(sides, axis=1)
            out = jnp.dot(high, rhs, preferred_element_type=F32) + jnp.dot(low, rhs, preferred_element_type=F32)
            out = out.astype(BF16)
            for half in range(2):
                start = pl.multiple_of(k * piece + g * 2 * CELLS_AT_ONCE + half * CELLS_AT_ONCE, CELLS_AT_ONCE)
                panels_ref[:, pl.ds(start, CELLS_AT_ONCE), :] = out[:, half * ens : (half + 1) * ens].reshape(
                    slices, CELLS_AT_ONCE, ens
                )
            return carry

        lax.fori_loop(0, piece // (2 * CELLS_AT_ONCE), group, 0, unroll=2)
    for k in range(LOADS // 2, LOADS):
        arrange(k)
    for k in range(PIECES):
        sends[k].wait_send()


def both(one, two):
    zero = jnp.zeros_like(one)
    return jnp.concatenate(
        [jnp.concatenate([one, zero], axis=1), jnp.concatenate([zero, two], axis=1)], axis=0
    )


def products(index_ref, left_ref, right_ref, acc, to, source):
    acc[...] = jnp.zeros_like(acc)
    ens = acc.shape[2]

    def body(g, carry):
        for j in range(PAIRS):
            pair = g * PAIRS + j
            one = right_ref[index_ref[source, 2 * pair]]
            two = right_ref[index_ref[source, 2 * pair + 1]]
            out = jnp.dot(left_ref[pair], both(one, two), preferred_element_type=F32)
            acc[index_ref[to, 2 * pair]] += out[:, :ens]
            acc[index_ref[to, 2 * pair + 1]] += out[:, ens:]
        return carry

    lax.fori_loop(0, left_ref.shape[0] // PAIRS, body, 0)


def forward_kernel(index_ref, pairs_ref, panels_ref, part_ref, acc):
    products(index_ref, pairs_ref, panels_ref, acc, 0, 1)
    part_ref[...] = acc[pl.ds(0, part_ref.shape[0])].astype(BF16)


def exchange_kernel(
    regions, part_ref, obs_ref, inv_ref, pairs_ref, all_ref, own_ref, turned_ref, got, send_a, recv_a, send_b, recv_b
):
    me = lax.axis_index("region")
    rows, ens = obs_ref.shape
    barrier = pltpu.get_barrier_semaphore()
    for k in range(1, regions):
        peer = lax.rem(me + k, regions)
        pl.semaphore_signal(barrier, inc=1, device_id={"region": peer}, device_id_type=MESH)
    row = lax.broadcasted_iota(jnp.int32, (rows, rows), 0)
    col = lax.broadcasted_iota(jnp.int32, (rows, rows), 1)
    inner = row % BLOCK
    half = BLOCK // 2
    picked = (row // BLOCK) * BLOCK + (inner % half) * 2 + inner // half == col
    table = picked.astype(BF16)
    obs = jnp.dot(table, obs_ref[...], preferred_element_type=F32)
    inv = jnp.sum(jnp.where(picked, inv_ref[...], 0.0), axis=1, keepdims=True)
    pl.semaphore_wait(barrier, regions - 1)

    def first(k):
        peer = lax.rem(me + k, regions)
        return pltpu.make_async_remote_copy(
            src_ref=part_ref.at[peer],
            dst_ref=got.at[k],
            send_sem=send_a.at[k],
            recv_sem=recv_a.at[k],
            device_id={"region": peer},
            device_id_type=MESH,
        )

    def second(k):
        peer = lax.rem(me + k, regions)
        return pltpu.make_async_remote_copy(
            src_ref=all_ref.at[me],
            dst_ref=all_ref.at[me],
            send_sem=send_b.at[k],
            recv_sem=recv_b.at[k],
            device_id={"region": peer},
            device_id_type=MESH,
        )

    firsts = [first(k) for k in range(1, regions)]
    for copy in firsts:
        copy.start()

    pair_count = pairs_ref.shape[0]

    def turn(g, carry):
        for j in range(TURNS):
            x = pairs_ref[g * TURNS + j]
            stacked = jnp.concatenate([x, halves_swapped(x)], axis=0)
            turned_ref[g * TURNS + j] = stacked.T[:BLOCK]
        return carry

    lax.fori_loop(0, pair_count // TURNS // 2, turn, 0)
    evolved = part_ref[me].astype(F32)
    for k in range(1, regions):
        firsts[k - 1].wait_recv()
        evolved = evolved + got[k].astype(F32)
    misfit = (inv * (evolved - obs)).astype(BF16)
    all_ref[me] = misfit
    seconds = [second(k) for k in range(1, regions)]
    for copy in seconds:
        copy.start()
    own_ref[...] = lax.dot_general(
        table, misfit, (((0,), (0,)), ((), ())), preferred_element_type=F32
    ).astype(BF16)
    for copy in firsts:
        copy.wait_send()
    lax.fori_loop(pair_count // TURNS // 2, pair_count // TURNS, turn, 0)
    for k in range(1, regions):
        source = lax.rem(me - k + regions, regions)
        pltpu.make_async_remote_copy(
            src_ref=all_ref.at[source],
            dst_ref=all_ref.at[source],
            send_sem=send_b.at[k],
            recv_sem=recv_b.at[k],
            device_id={"region": source},
            device_id_type=MESH,
        ).wait_recv()
    for copy in seconds:
        copy.wait_send()


def adjoint_kernel(index_ref, turned_ref, misfit_ref, own_ref, acc, misfit_out):
    products(index_ref, turned_ref, misfit_ref, acc, 2, 3)
    misfit_out[...] = own_ref[...]


def gradient_kernel(acc_ref, blend_ref, mix_ref, grad_ref, mine, away, got, send_sem, recv_sem):
    me = lax.axis_index("window")
    other = 1 - me
    slabs, cells, ens = grad_ref.shape
    slices = 2 * slabs
    blocks = cells // BLOCK
    barrier = pltpu.get_barrier_semaphore()
    pl.semaphore_signal(barrier, inc=1, device_id={"window": other}, device_id_type=MESH)
    high, low = spread(blend_ref[...], CELLS_AT_ONCE)
    mix = mix_ref[...]
    pl.semaphore_wait(barrier, 1)

    def send(block):
        return pltpu.make_async_remote_copy(
            src_ref=away.at[block],
            dst_ref=got.at[block],
            send_sem=send_sem.at[block],
            recv_sem=recv_sem.at[block],
            device_id={"window": other},
            device_id_type=MESH,
        )

    def pull(block):
        for within in range(BLOCK // (2 * CELLS_AT_ONCE)):
            sides = []
            for half in range(2):
                start = (2 * within + half) * CELLS_AT_ONCE
                rows = [acc_ref[t * blocks + block, pl.ds(start, CELLS_AT_ONCE), :] for t in range(slices)]
                sides.append(jnp.concatenate(rows, axis=0))
            rhs = jnp.concatenate(sides, axis=1)
            rhs_high = rhs.astype(BF16)
            rhs_low = (rhs - rhs_high.astype(F32)).astype(BF16)
            dims = (((0,), (0,)), ((), ()))
            out = lax.dot_general(high, rhs_high, dims, preferred_element_type=F32)
            out = out + lax.dot_general(low, rhs_high, dims, preferred_element_type=F32)
            out = (out + lax.dot_general(high, rhs_low, dims, preferred_element_type=F32)).astype(BF16)
            for half in range(2):
                start = (2 * within + half) * CELLS_AT_ONCE
                piece = out[:, half * ens : (half + 1) * ens].reshape(slices, CELLS_AT_ONCE, ens)
                first, second = piece[:slabs], piece[slabs:]
                mine[block, :, pl.ds(start, CELLS_AT_ONCE), :] = jnp.where(me == 0, first, second)
                away[block, :, pl.ds(start, CELLS_AT_ONCE), :] = jnp.where(me == 0, second, first)

    def finish(block):
        send(block).wait_recv()
        total = (mine[block].astype(F32) + got[block].astype(F32)).astype(BF16).reshape(slabs * BLOCK, ens)
        grad = jnp.dot(total, mix, preferred_element_type=F32).astype(BF16)
        grad_ref[:, pl.ds(block * BLOCK, BLOCK), :] = grad.reshape(slabs, BLOCK, ens)

    for block in range(blocks):
        pull(block)
        send(block).start()
        if block >= LAG:
            finish(block - LAG)
    for block in range(blocks - LAG, blocks):
        finish(block)
    for block in range(blocks):
        send(block).wait_send()


def vmem():
    return pl.BlockSpec(memory_space=pltpu.VMEM)


def shards(
    regions,
    flux,
    blend,
    footprints,
    receptor_block,
    cell_block,
    slice_index,
    live_counts,
    observed,
    inv_var,
    prior_mix,
):
    slabs, cells, ens = flux.shape
    slices = blend.shape[0]
    cell_blocks = cells // BLOCK
    panel_total = slices * cell_blocks
    slots = footprints.shape[1]
    rows = observed.shape[1]
    own_blocks = rows // BLOCK
    window_blocks = own_blocks * regions

    panels, pairs, index = pl.pallas_call(
        functools.partial(blend_kernel, window_blocks),
        out_shape=(
            jax.ShapeDtypeStruct((slices, cells, ens), BF16),
            jax.ShapeDtypeStruct((slots // 2, BLOCK, 2 * BLOCK), BF16),
            jax.ShapeDtypeStruct((4, slots), jnp.int32),
        ),
        in_specs=[vmem()] * 4 + [pl.BlockSpec(memory_space=pltpu.HBM)] * 3,
        out_specs=(vmem(), vmem(), vmem()),
        scratch_shapes=[
            pltpu.VMEM((slices, cells, ens), BF16),
            pltpu.VMEM((slots, BLOCK * BLOCK), BF16),
            pltpu.VMEM((slices, slices), F32),
            pltpu.SemaphoreType.DMA,
            pltpu.SemaphoreType.DMA((LOADS,)),
            pltpu.SemaphoreType.DMA((PIECES,)),
            pltpu.SemaphoreType.DMA((PIECES,)),
            pltpu.SemaphoreType.DMA((PIECES,)),
        ],
        compiler_params=pltpu.CompilerParams(collective_id=0, has_side_effects=True, vmem_limit_bytes=32 << 20),
        name="blend_slices",
    )(receptor_block, cell_block, slice_index, live_counts, blend, flux, footprints)

    smem = pl.BlockSpec(memory_space=pltpu.SMEM)
    part = pl.pallas_call(
        forward_kernel,
        out_shape=jax.ShapeDtypeStruct((window_blocks, BLOCK, ens), BF16),
        in_specs=[smem, vmem(), vmem()],
        out_specs=vmem(),
        scratch_shapes=[pltpu.VMEM((window_blocks + 1, BLOCK, ens), F32)],
        compiler_params=pltpu.CompilerParams(vmem_limit_bytes=32 << 20),
        name="forward_blocks",
    )(index, pairs, panels.reshape(panel_total, BLOCK, ens))

    misfit_all, own, turned = pl.pallas_call(
        functools.partial(exchange_kernel, regions),
        out_shape=(
            jax.ShapeDtypeStruct((regions, rows, ens), BF16),
            jax.ShapeDtypeStruct((rows, ens), BF16),
            jax.ShapeDtypeStruct((slots // 2, BLOCK, 2 * BLOCK), BF16),
        ),
        in_specs=[vmem()] * 4,
        out_specs=(vmem(), vmem(), vmem()),
        scratch_shapes=[
            pltpu.VMEM((regions, rows, ens), BF16),
            pltpu.SemaphoreType.DMA((regions,)),
            pltpu.SemaphoreType.DMA((regions,)),
            pltpu.SemaphoreType.DMA((regions,)),
            pltpu.SemaphoreType.DMA((regions,)),
        ],
        compiler_params=pltpu.CompilerParams(collective_id=1, has_side_effects=True, vmem_limit_bytes=32 << 20),
        name="misfit_exchange",
    )(part.reshape(regions, rows, ens), observed[0], inv_var, pairs)

    collected, misfit = pl.pallas_call(
        adjoint_kernel,
        out_shape=(
            jax.ShapeDtypeStruct((panel_total + 1, BLOCK, ens), F32),
            jax.ShapeDtypeStruct((rows, ens), BF16),
        ),
        in_specs=[smem, vmem(), vmem(), vmem()],
        out_specs=(vmem(), vmem()),
        compiler_params=pltpu.CompilerParams(vmem_limit_bytes=32 << 20),
        name="adjoint_blocks",
    )(index, turned, misfit_all.reshape(window_blocks, BLOCK, ens), own)

    blocks_shape = (cell_blocks, slabs, BLOCK, ens)
    gradient = pl.pallas_call(
        gradient_kernel,
        out_shape=jax.ShapeDtypeStruct((slabs, cells, ens), BF16),
        in_specs=[vmem(), vmem(), vmem()],
        out_specs=vmem(),
        scratch_shapes=[
            pltpu.VMEM(blocks_shape, BF16),
            pltpu.VMEM(blocks_shape, BF16),
            pltpu.VMEM(blocks_shape, BF16),
            pltpu.SemaphoreType.DMA((cell_blocks,)),
            pltpu.SemaphoreType.DMA((cell_blocks,)),
        ],
        compiler_params=pltpu.CompilerParams(collective_id=2, has_side_effects=True, vmem_limit_bytes=32 << 20),
        name="gradient_exchange",
    )(collected, blend, prior_mix)
    return misfit[None], gradient


def solution(mesh):
    in_specs = (
        P(("group", "window"), "region", None),
        P(),
        P(("group", "window"), "region", None),
        P(("group", "window"), "region"),
        P(("group", "window"), "region"),
        P(("group", "window"), "region"),
        P(("group", "window"), "region"),
        P(("group", "window"), "region", None),
        P(("group", "window"), "region"),
        P(),
    )
    out_specs = (P(("group", "window"), "region", None), P(("group", "window"), "region", None))
    return jax.shard_map(
        functools.partial(shards, mesh.shape["region"]),
        mesh=mesh,
        in_specs=in_specs,
        out_specs=out_specs,
        check_vma=False,
    )
```

time: 83.7 us -> 94.3 us (1.13)
  local copies, waits for them, and re-layouts: 6.9 us -> 14.9 us
  Pallas kernels: 73.5 us -> 77.2 us
  other arithmetic: 1.4 us -> 0 us
    unnamed x16 -> x25, local copies, waits for them, and re-layouts: 6.9 us -> 14.9 us
    pallas_call x1, Pallas kernels: 18.6 us -> 22.4 us  [shards(): pl.pallas_call(functools.partial(exchange_kernel, regions), out_shape=(ja...]
    pallas_call x3, Pallas kernels: 51.7 us -> 48.9 us  [the longest x1 18.4 us: shards(): pl.pallas_call(adjoint_kernel, out_shape=(jax.ShapeDtypeStruct((panel_tot...]
    pallas_call x1, Pallas kernels: 3.14 us -> 5.82 us  [shards(): pl.pallas_call(gradient_kernel, out_shape=jax.ShapeDtypeStruct((slabs, ce...]
where the time goes in v2:
time: 94.3 us; the launch traced here: 93.5 us
  Pallas kernels  77.2 us (82%)
  local copies, waits for them, and re-layouts  14.9 us (16%)
  between operations  1.37 us (1%)
    pallas_call x1, Pallas kernels, shards(): pl.pallas_call(functools.partial(exchange_kernel, regions), out_shape=(ja...  22.4 us
    pallas_call x1, Pallas kernels, shards(): pl.pallas_call(adjoint_kernel, out_shape=(jax.ShapeDtypeStruct((panel_tot...  18.4 us
    pallas_call x1, Pallas kernels, shards(): pl.pallas_call(forward_kernel, out_shape=jax.ShapeDtypeStruct((window_blo...  17.9 us
    unnamed x25, local copies, waits for them, and re-layouts  14.9 us
    pallas_call x1, Pallas kernels, shards(): pl.pallas_call(functools.partial(blend_kernel, window_blocks), out_shape=...  12.6 us
    pallas_call x1, Pallas kernels, shards(): pl.pallas_call(gradient_kernel, out_shape=jax.ShapeDtypeStruct((slabs, ce...  5.82 us

profile of v2, /device:TPU:0, one launch (start us, length us, event | category | flops | bytes accessed | tf_op | source)
XLA Modules:
  0.0 93.5 jit_solution(14384154986357448013)
XLA Ops:
  1.3 0.0 copy-start
  1.3 3.4 %copy-done = bf16[1,1024,4096]{2,1,0:T(8,128)(2,1)S(1)} copy-done((bf16[1,1024,4096]{2,1,0:T(8,128)(2,1)S(1)}, bf16[1,1024,4096]{2,1,0:T(8,128)(2,1)}, u32[]{:S(2)}) %copy-start) | copy-done | bytes 8388632
  4.7 0.0 copy-start.3
  4.7 1.2 %copy-done.3 = bf16[8,512,128]{2,1,0:T(8,128)(2,1)S(1)} copy-done((bf16[8,512,128]{2,1,0:T(8,128)(2,1)S(1)}, bf16[8,512,128]{2,1,0:T(8,128)(2,1)}, u32[]{:S(2)}) %copy-start.3) | copy-done | bytes 1048600
  5.9 0.0 copy-start.6
  5.9 0.7 copy-done.6
  6.6 0.0 copy-start.8
  6.6 0.7 copy-done.8
  7.3 0.0 copy-start.9
  7.3 0.7 copy-done.9
  8.0 0.0 copy-start.10
  8.0 0.7 copy-done.10
  8.6 0.0 copy-start.4
  8.6 0.0 copy-start.11
  8.6 12.6 %blend_slices.1 = (bf16[16,512,128]{2,1,0:T(8,128)(2,1)S(1)}, bf16[512,64,128]{2,1,0:T(8,128)(2,1)S(1)}, s32[4,1024]{1,0:T(4,128)S(1)}) custom-call(s32[1,1024]{1,0:T(1,128)S(1)} %copy-done.8, s32[1,1024]{1,0:T(1,128)S(1)} %copy-done.9, s32[1,1024]{1,0:T(1,128)S(1)} %copy-done.10, s32[1,1]{1,0:T(1,128)S(6)} %copy.13.live_ref, f32[16,16]{1,0:T(8,128)S(1)} %copy-done.6, ...), custom_call_target="tpu_custom_call" | custom-call | tf_op jit(solution)/shard_map/blend_slices/pallas_call | solution.py:366
  21.3 17.9 %forward_blocks.1 = bf16[16,64,128]{2,1,0:T(8,128)(2,1)S(1)} custom-call(s32[4,1024]{1,0:T(4,128)S(1)} %get-tuple-element.10.index_ref, bf16[512,64,128]{2,1,0:T(8,128)(2,1)S(1)} %get-tuple-element.11.pairs_ref, bf16[128,64,128]{2,1,0:T(8,128)(2,1)S(1)} %bitcast.5), custom_call_target="tpu_custom_call" | custom-call | tf_op jit(solution)/shard_map/forward_blocks/pallas_call | solution.py:390
  39.2 0.0 copy-done.4
  39.2 0.0 copy-done.11
  39.2 0.0 copy-start.5
  39.2 0.0 copy-start.7
  39.2 22.4 %misfit_exchange.1 = (bf16[8,128,128]{2,1,0:T(8,128)(2,1)S(1)}, bf16[128,128]{1,0:T(8,128)(2,1)S(1)}, bf16[512,64,128]{2,1,0:T(8,128)(2,1)S(1)}) custom-call(bf16[8,128,128]{2,1,0:T(8,128)(2,1)S(1)} %bitcast.6, bf16[128,128]{1,0:T(8,128)(2,1)S(1)} %bitcast.8, f32[1,128]{1,0:T(1,128)S(1)} %copy-done.11, bf16[512,64,128]{2,1,0:T(8,128)(2,1)S(1)} %get-tuple-element.11.pairs_ref), custom_call_target="tpu_custom_call" | custom-call | tf_op jit(solution)/shard_map/misfit_exchange/pallas_call | solution.py:400
  61.6 0.0 copy-start.1
  61.7 3.2 %copy-done.1 = bf16[512,64,128]{2,1,0:T(8,128)(2,1)} copy-done((bf16[512,64,128]{2,1,0:T(8,128)(2,1)}, bf16[512,64,128]{2,1,0:T(8,128)(2,1)S(1)}, u32[]{:S(2)}) %copy-start.1) | copy-done | bytes 8388632
  64.9 0.0 copy-start.2
  64.9 3.4 %copy-done.2 = bf16[512,64,128]{2,1,0:T(8,128)(2,1)S(1)} copy-done((bf16[512,64,128]{2,1,0:T(8,128)(2,1)S(1)}, bf16[512,64,128]{2,1,0:T(8,128)(2,1)}, u32[]{:S(2)}) %copy-start.2) | copy-done | bytes 8388632
  68.3 18.4 %adjoint_blocks.1 = (f32[129,64,128]{2,1,0:T(8,128)S(1)}, bf16[128,128]{1,0:T(8,128)(2,1)}) custom-call(s32[4,1024]{1,0:T(4,128)S(1)} %get-tuple-element.10.index_ref, bf16[512,64,128]{2,1,0:T(8,128)(2,1)S(1)} %copy-done.2, bf16[16,64,128]{2,1,0:T(8,128)(2,1)S(1)} %bitcast.7, bf16[128,128]{1,0:T(8,128)(2,1)S(1)} %get-tuple-element.15.own_ref), custom_call_target="tpu_custom_call" | custom-call | tf_op jit(solution)/shard_map/adjoint_blocks/pallas_call | solution.py:420
  86.7 0.0 copy-done.5
  86.7 0.0 copy-done.7
  86.7 5.8 %gradient_exchange.1 = bf16[8,512,128]{2,1,0:T(8,128)(2,1)S(1)} custom-call(f32[129,64,128]{2,1,0:T(8,128)S(1)} %get-tuple-element.17.acc_ref, f32[16,16]{1,0:T(8,128)S(1)} %copy-done.7, bf16[128,128]{1,0:T(8,128)(2,1)S(1)} %copy-done.5), custom_call_target="tpu_custom_call" | custom-call | tf_op jit(solution)/shard_map/gradient_exchange/pallas_call | solution.py:433
  92.5 1.0 %copy.14 = bf16[8,512,128]{2,1,0:T(8,128)(2,1)} copy(bf16[8,512,128]{2,1,0:T(8,128)(2,1)S(1)} %gradient_exchange.1) | data formatting | bytes 2097152
Async XLA Ops:
  1.3 3.4 %copy-start = (bf16[1,1024,4096]{2,1,0:T(8,128)(2,1)S(1)}, bf16[1,1024,4096]{2,1,0:T(8,128)(2,1)}, u32[]{:S(2)}) copy-start(bf16[1,1024,4096]{2,1,0:T(8,128)(2,1)} %fp_hbm.1) | copy-start | bytes 25165828
  4.7 1.2 %copy-start.3 = (bf16[8,512,128]{2,1,0:T(8,128)(2,1)S(1)}, bf16[8,512,128]{2,1,0:T(8,128)(2,1)}, u32[]{:S(2)}) copy-start(bf16[8,512,128]{2,1,0:T(8,128)(2,1)} %flux_hbm.1) | copy-start | bytes 3145732
  5.9 0.7 copy-start.6
  6.6 0.7 copy-start.8
  7.3 0.7 copy-start.9
  8.0 0.7 copy-start.10
  8.6 30.6 %copy-start.4 = (bf16[1,128,128]{2,1,0:T(8,128)(2,1)S(1)}, bf16[1,128,128]{2,1,0:T(8,128)(2,1)}, u32[]{:S(2)}) copy-start(bf16[1,128,128]{2,1,0:T(8,128)(2,1)} %param.17) | copy-start | bytes 98308
  8.6 30.6 %copy-start.11 = (f32[1,128]{1,0:T(1,128)S(1)}, f32[1,128]{1,0:T(1,128)}, u32[]{:S(2)}) copy-start(f32[1,128]{1,0:T(1,128)} %inv_ref.1) | copy-start | bytes 1540
  39.2 47.4 %copy-start.5 = (bf16[128,128]{1,0:T(8,128)(2,1)S(1)}, bf16[128,128]{1,0:T(8,128)(2,1)}, u32[]{:S(2)}) copy-start(bf16[128,128]{1,0:T(8,128)(2,1)} %mix_ref.1) | copy-start | bytes 98308
  39.2 47.4 %copy-start.7 = (f32[16,16]{1,0:T(8,128)S(1)}, f32[16,16]{1,0:T(8,128)}, u32[]{:S(2)}) copy-start(f32[16,16]{1,0:T(8,128)} %blend_ref.1) | copy-start | bytes 3076
  61.6 3.2 %copy-start.1 = (bf16[512,64,128]{2,1,0:T(8,128)(2,1)}, bf16[512,64,128]{2,1,0:T(8,128)(2,1)S(1)}, u32[]{:S(2)}) copy-start(bf16[512,64,128]{2,1,0:T(8,128)(2,1)S(1)} %get-tuple-element.13.turned_ref) | copy-start | bytes 25165828
  64.9 3.4 %copy-start.2 = (bf16[512,64,128]{2,1,0:T(8,128)(2,1)S(1)}, bf16[512,64,128]{2,1,0:T(8,128)(2,1)}, u32[]{:S(2)}) copy-start(bf16[512,64,128]{2,1,0:T(8,128)(2,1)} %copy-done.1) | copy-start | bytes 25165828

commit v3 on v2

--- a/solution.py
+++ b/solution.py
@@ -12,11 +12,12 @@
 F32 = jnp.float32
 BF16 = jnp.bfloat16
 SUB = 16
+SUBS = 4
 CELLS_AT_ONCE = 16
 PIECES = 4
 LOADS = 8
-PAIRS = 8
-TURNS = 8
+PAIRS = 32
+TURNS = 32
 LAG = 2
 
 
@@ -45,9 +46,9 @@
 
 def blend_kernel(
     window_blocks,
-    recv_ref,
-    cell_ref,
-    slice_ref,
+    recv_hbm,
+    cell_hbm,
+    slice_hbm,
     live_ref,
     blend_hbm,
     flux_hbm,
@@ -58,7 +59,10 @@
     full,
     raw,
     blend_ref,
-    blend_sem,
+    recv_ref,
+    cell_ref,
+    slice_ref,
+    small_sem,
     fp_sem,
     local_sem,
     send_sem,
@@ -71,8 +75,14 @@
     slots = raw.shape[0]
     barrier = pltpu.get_barrier_semaphore()
     pl.semaphore_signal(barrier, inc=1, device_id={"window": other}, device_id_type=MESH)
-    blend_copy = pltpu.make_async_copy(blend_hbm, blend_ref, blend_sem)
-    blend_copy.start()
+    smalls = [
+        pltpu.make_async_copy(source, target, small_sem.at[k])
+        for k, (source, target) in enumerate(
+            ((blend_hbm, blend_ref), (recv_hbm, recv_ref), (cell_hbm, cell_ref), (slice_hbm, slice_ref))
+        )
+    ]
+    for copy in smalls:
+        copy.start()
     piece = cells // PIECES
     locals_, sends, loads = [], [], []
     for k in range(PIECES):
@@ -105,6 +115,8 @@
     for k in range(1, LOADS):
         loads[k].start()
 
+    for copy in smalls:
+        copy.wait()
     cell_blocks = cells // BLOCK
     live = lax.broadcasted_iota(jnp.int32, recv_ref.shape, 1) < live_ref[...]
     panel = slice_ref[...] * cell_blocks + cell_ref[...]
@@ -112,24 +124,25 @@
     index_ref[pl.ds(1, 1), :] = jnp.where(live, panel, 0)
     index_ref[pl.ds(2, 1), :] = jnp.where(live, panel, slices * cell_blocks)
     index_ref[pl.ds(3, 1), :] = jnp.where(live, recv_ref[...], 0)
-    blend_copy.wait()
     high, low = spread(blend_ref[...], CELLS_AT_ONCE)
 
     def arrange(k):
         loads[k].wait()
 
         def body(g, carry):
-            base = pl.multiple_of(k * part + g * SUB, SUB)
-            x = raw[pl.ds(base, SUB), :].reshape(SUB, BLOCK // 2, 2 * BLOCK)
             lower = lax.broadcasted_iota(jnp.int32, (BLOCK // 2, 2 * BLOCK), 1) < BLOCK
-            for j in range(0, SUB, 2):
-                one, two = x[j], x[j + 1]
-                even = jnp.where(lower, one, halves_swapped(two))
-                odd = jnp.where(lower, halves_swapped(one), two)
-                pairs_ref[k * (part // 2) + g * (SUB // 2) + j // 2] = jnp.concatenate([even, odd], axis=0)
+            for sub in range(SUBS):
+                base = pl.multiple_of(k * part + g * SUBS * SUB + sub * SUB, SUB)
+                x = raw[pl.ds(base, SUB), :].reshape(SUB, BLOCK // 2, 2 * BLOCK)
+                for j in range(0, SUB, 2):
+                    one, two = x[j], x[j + 1]
+                    even = jnp.where(lower, one, halves_swapped(two))
+                    odd = jnp.where(lower, halves_swapped(one), two)
+                    place = k * (part // 2) + (g * SUBS + sub) * (SUB // 2) + j // 2
+                    pairs_ref[place] = jnp.concatenate([even, odd], axis=0)
             return carry
 
-        lax.fori_loop(0, part // SUB, body, 0)
+        lax.fori_loop(0, part // SUB // SUBS, body, 0)
 
     for k in range(LOADS // 2):
         arrange(k)
@@ -341,6 +354,14 @@
     return pl.BlockSpec(memory_space=pltpu.VMEM)
 
 
+def hbm():
+    return pl.BlockSpec(memory_space=pltpu.HBM)
+
+
+def stay(x):
+    return pltpu.with_memory_space_constraint(x, pltpu.HBM)
+
+
 def shards(
     regions,
     flux,
@@ -370,21 +391,32 @@
             jax.ShapeDtypeStruct((slots // 2, BLOCK, 2 * BLOCK), BF16),
             jax.ShapeDtypeStruct((4, slots), jnp.int32),
         ),
-        in_specs=[vmem()] * 4 + [pl.BlockSpec(memory_space=pltpu.HBM)] * 3,
+        in_specs=[hbm()] * 3 + [vmem()] + [hbm()] * 3,
         out_specs=(vmem(), vmem(), vmem()),
         scratch_shapes=[
             pltpu.VMEM((slices, cells, ens), BF16),
             pltpu.VMEM((slots, BLOCK * BLOCK), BF16),
             pltpu.VMEM((slices, slices), F32),
-            pltpu.SemaphoreType.DMA,
+            pltpu.VMEM((1, slots), jnp.int32),
+            pltpu.VMEM((1, slots), jnp.int32),
+            pltpu.VMEM((1, slots), jnp.int32),
+            pltpu.SemaphoreType.DMA((4,)),
             pltpu.SemaphoreType.DMA((LOADS,)),
             pltpu.SemaphoreType.DMA((PIECES,)),
             pltpu.SemaphoreType.DMA((PIECES,)),
             pltpu.SemaphoreType.DMA((PIECES,)),
         ],
-        compiler_params=pltpu.CompilerParams(collective_id=0, has_side_effects=True, vmem_limit_bytes=32 << 20),
+        compiler_params=pltpu.CompilerParams(collective_id=0, has_side_effects=True, vmem_limit_bytes=24 << 20),
         name="blend_slices",
-    )(receptor_block, cell_block, slice_index, live_counts, blend, flux, footprints)
+    )(
+        stay(receptor_block),
+        stay(cell_block),
+        stay(slice_index),
+        live_counts,
+        stay(blend),
+        stay(flux),
+        stay(footprints),
+    )
 
     smem = pl.BlockSpec(memory_space=pltpu.SMEM)
     part = pl.pallas_call(
@@ -393,7 +425,7 @@
         in_specs=[smem, vmem(), vmem()],
         out_specs=vmem(),
         scratch_shapes=[pltpu.VMEM((window_blocks + 1, BLOCK, ens), F32)],
-        compiler_params=pltpu.CompilerParams(vmem_limit_bytes=32 << 20),
+        compiler_params=pltpu.CompilerParams(vmem_limit_bytes=16 << 20),
         name="forward_blocks",
     )(index, pairs, panels.reshape(panel_total, BLOCK, ens))
 
@@ -413,7 +445,7 @@
             pltpu.SemaphoreType.DMA((regions,)),
             pltpu.SemaphoreType.DMA((regions,)),
         ],
-        compiler_params=pltpu.CompilerParams(collective_id=1, has_side_effects=True, vmem_limit_bytes=32 << 20),
+        compiler_params=pltpu.CompilerParams(collective_id=1, has_side_effects=True, vmem_limit_bytes=16 << 20),
         name="misfit_exchange",
     )(part.reshape(regions, rows, ens), observed[0], inv_var, pairs)
 
@@ -425,7 +457,7 @@
         ),
         in_specs=[smem, vmem(), vmem(), vmem()],
         out_specs=(vmem(), vmem()),
-        compiler_params=pltpu.CompilerParams(vmem_limit_bytes=32 << 20),
+        compiler_params=pltpu.CompilerParams(vmem_limit_bytes=16 << 20),
         name="adjoint_blocks",
     )(index, turned, misfit_all.reshape(window_blocks, BLOCK, ens), own)
 
@@ -442,7 +474,7 @@
             pltpu.SemaphoreType.DMA((cell_blocks,)),
             pltpu.SemaphoreType.DMA((cell_blocks,)),
         ],
-        compiler_params=pltpu.CompilerParams(collective_id=2, has_side_effects=True, vmem_limit_bytes=32 << 20),
+        compiler_params=pltpu.CompilerParams(collective_id=2, has_side_effects=True, vmem_limit_bytes=16 << 20),
         name="gradient_exchange",
     )(collected, blend, prior_mix)
     return misfit[None], gradient

time: 94.3 us -> 65.4 us (0.69)
  Pallas kernels: 77.2 us -> 62.9 us
  local copies, waits for them, and re-layouts: 14.9 us -> 0.99 us
    unnamed x25 -> x9, local copies, waits for them, and re-layouts: 14.9 us -> 0.99 us
    pallas_call x1, Pallas kernels: 17.9 us -> 10.6 us  [shards(): pl.pallas_call(forward_kernel, out_shape=jax.ShapeDtypeStruct((window_blo...]
    pallas_call x1, Pallas kernels: 18.4 us -> 11.6 us  [shards(): pl.pallas_call(adjoint_kernel, out_shape=(jax.ShapeDtypeStruct((panel_tot...]
    pallas_call x1, Pallas kernels: 22.4 us -> 25.6 us  [shards(): pl.pallas_call(functools.partial(exchange_kernel, regions), out_shape=(ja...]
    pallas_call x1, Pallas kernels: 12.6 us -> 9.43 us  [shards(): pl.pallas_call(functools.partial(blend_kernel, window_blocks), out_shape=...]
where the time goes in v3:
time: 65.4 us; the launch traced here: 65.2 us
  Pallas kernels  62.9 us (96%)
  between operations  1.36 us (2%)
  local copies, waits for them, and re-layouts  0.99 us (2%)
    pallas_call x1, Pallas kernels, shards(): pl.pallas_call(functools.partial(exchange_kernel, regions), out_shape=(ja...  25.6 us
    pallas_call x1, Pallas kernels, shards(): pl.pallas_call(adjoint_kernel, out_shape=(jax.ShapeDtypeStruct((panel_tot...  11.6 us
    pallas_call x1, Pallas kernels, shards(): pl.pallas_call(forward_kernel, out_shape=jax.ShapeDtypeStruct((window_blo...  10.6 us
    pallas_call x1, Pallas kernels, shards(): pl.pallas_call(functools.partial(blend_kernel, window_blocks), out_shape=...  9.43 us
    pallas_call x1, Pallas kernels, shards(): pl.pallas_call(gradient_kernel, out_shape=jax.ShapeDtypeStruct((slabs, ce...  5.6 us

profile of v3, /device:TPU:0, one launch (start us, length us, event | category | flops | bytes accessed | tf_op | source)
XLA Modules:
  0.0 65.2 jit_solution(9441538213996691927)
XLA Ops:
  1.3 0.0 copy-start
  1.3 0.0 copy-start.3
  1.3 9.4 %blend_slices.1 = (bf16[16,512,128]{2,1,0:T(8,128)(2,1)S(1)}, bf16[512,64,128]{2,1,0:T(8,128)(2,1)S(1)}, s32[4,1024]{1,0:T(4,128)S(1)}) custom-call(s32[1,1024]{1,0:T(1,128)} %recv_hbm.1, s32[1,1024]{1,0:T(1,128)} %cell_hbm.1, s32[1,1024]{1,0:T(1,128)} %slice_hbm.1, s32[1,1]{1,0:T(1,128)S(6)} %copy.13.live_ref, f32[16,16]{1,0:T(8,128)} %blend_ref.1, ...), custom_call_target="tpu_custom_call" | custom-call | tf_op jit(solution)/shard_map/blend_slices/pallas_call | solution.py:387
  10.7 10.6 %forward_blocks.1 = bf16[16,64,128]{2,1,0:T(8,128)(2,1)S(1)} custom-call(s32[4,1024]{1,0:T(4,128)S(1)} %get-tuple-element.10.index_ref, bf16[512,64,128]{2,1,0:T(8,128)(2,1)S(1)} %get-tuple-element.11.pairs_ref, bf16[128,64,128]{2,1,0:T(8,128)(2,1)S(1)} %bitcast.5), custom_call_target="tpu_custom_call" | custom-call | tf_op jit(solution)/shard_map/forward_blocks/pallas_call | solution.py:422
  21.4 0.0 copy-done
  21.4 0.0 copy-done.3
  21.4 0.0 copy-start.1
  21.4 0.0 copy-start.2
  21.4 25.6 %misfit_exchange.1 = (bf16[8,128,128]{2,1,0:T(8,128)(2,1)S(1)}, bf16[128,128]{1,0:T(8,128)(2,1)S(1)}, bf16[512,64,128]{2,1,0:T(8,128)(2,1)S(1)}) custom-call(bf16[8,128,128]{2,1,0:T(8,128)(2,1)S(1)} %bitcast.6, bf16[128,128]{1,0:T(8,128)(2,1)S(1)} %bitcast.8, f32[1,128]{1,0:T(1,128)S(1)} %copy-done.3, bf16[512,64,128]{2,1,0:T(8,128)(2,1)S(1)} %get-tuple-element.11.pairs_ref), custom_call_target="tpu_custom_call" | custom-call | tf_op jit(solution)/shard_map/misfit_exchange/pallas_call | solution.py:432
  47.0 11.6 %adjoint_blocks.1 = (f32[129,64,128]{2,1,0:T(8,128)S(1)}, bf16[128,128]{1,0:T(8,128)(2,1)}) custom-call(s32[4,1024]{1,0:T(4,128)S(1)} %get-tuple-element.10.index_ref, bf16[512,64,128]{2,1,0:T(8,128)(2,1)S(1)} %get-tuple-element.13.turned_ref, bf16[16,64,128]{2,1,0:T(8,128)(2,1)S(1)} %bitcast.7, bf16[128,128]{1,0:T(8,128)(2,1)S(1)} %get-tuple-element.15.own_ref), custom_call_target="tpu_custom_call" | custom-call | tf_op jit(solution)/shard_map/adjoint_blocks/pallas_call | solution.py:452
  58.6 0.0 copy-done.1
  58.6 0.0 copy-done.2
  58.6 5.6 %gradient_exchange.1 = bf16[8,512,128]{2,1,0:T(8,128)(2,1)S(1)} custom-call(f32[129,64,128]{2,1,0:T(8,128)S(1)} %get-tuple-element.17.acc_ref, f32[16,16]{1,0:T(8,128)S(1)} %copy-done.2, bf16[128,128]{1,0:T(8,128)(2,1)S(1)} %copy-done.1), custom_call_target="tpu_custom_call" | custom-call | tf_op jit(solution)/shard_map/gradient_exchange/pallas_call | solution.py:465
  64.2 1.0 %copy.14 = bf16[8,512,128]{2,1,0:T(8,128)(2,1)} copy(bf16[8,512,128]{2,1,0:T(8,128)(2,1)S(1)} %gradient_exchange.1) | data formatting | bytes 2097152
Async XLA Ops:
  1.3 20.1 %copy-start = (bf16[1,128,128]{2,1,0:T(8,128)(2,1)S(1)}, bf16[1,128,128]{2,1,0:T(8,128)(2,1)}, u32[]{:S(2)}) copy-start(bf16[1,128,128]{2,1,0:T(8,128)(2,1)} %param.17) | copy-start | bytes 98308
  1.3 20.1 %copy-start.3 = (f32[1,128]{1,0:T(1,128)S(1)}, f32[1,128]{1,0:T(1,128)}, u32[]{:S(2)}) copy-start(f32[1,128]{1,0:T(1,128)} %inv_ref.1) | copy-start | bytes 1540
  21.4 37.3 %copy-start.1 = (bf16[128,128]{1,0:T(8,128)(2,1)S(1)}, bf16[128,128]{1,0:T(8,128)(2,1)}, u32[]{:S(2)}) copy-start(bf16[128,128]{1,0:T(8,128)(2,1)} %mix_ref.1) | copy-start | bytes 98308
  21.4 37.2 %copy-start.2 = (f32[16,16]{1,0:T(8,128)S(1)}, f32[16,16]{1,0:T(8,128)}, u32[]{:S(2)}) copy-start(f32[16,16]{1,0:T(8,128)} %blend_ref.1) | copy-start | bytes 3076

commit v4 on v3

--- a/solution.py
+++ b/solution.py
@@ -54,10 +54,9 @@
     flux_hbm,
     fp_hbm,
     panels_ref,
-    pairs_ref,
+    raw,
     index_ref,
     full,
-    raw,
     blend_ref,
     recv_ref,
     cell_ref,
@@ -126,26 +125,6 @@
     index_ref[pl.ds(3, 1), :] = jnp.where(live, recv_ref[...], 0)
     high, low = spread(blend_ref[...], CELLS_AT_ONCE)
 
-    def arrange(k):
-        loads[k].wait()
-
-        def body(g, carry):
-            lower = lax.broadcasted_iota(jnp.int32, (BLOCK // 2, 2 * BLOCK), 1) < BLOCK
-            for sub in range(SUBS):
-                base = pl.multiple_of(k * part + g * SUBS * SUB + sub * SUB, SUB)
-                x = raw[pl.ds(base, SUB), :].reshape(SUB, BLOCK // 2, 2 * BLOCK)
-                for j in range(0, SUB, 2):
-                    one, two = x[j], x[j + 1]
-                    even = jnp.where(lower, one, halves_swapped(two))
-                    odd = jnp.where(lower, halves_swapped(one), two)
-                    place = k * (part // 2) + (g * SUBS + sub) * (SUB // 2) + j // 2
-                    pairs_ref[place] = jnp.concatenate([even, odd], axis=0)
-            return carry
-
-        lax.fori_loop(0, part // SUB // SUBS, body, 0)
-
-    for k in range(LOADS // 2):
-        arrange(k)
     for k in range(PIECES):
         locals_[k].wait()
         sends[k].wait_recv()
@@ -166,10 +145,10 @@
             return carry
 
         lax.fori_loop(0, piece // (2 * CELLS_AT_ONCE), group, 0, unroll=2)
-    for k in range(LOADS // 2, LOADS):
-        arrange(k)
     for k in range(PIECES):
         sends[k].wait_send()
+    for copy in loads:
+        copy.wait()
 
 
 def both(one, two):
@@ -179,30 +158,51 @@
     )
 
 
-def products(index_ref, left_ref, right_ref, acc, to, source):
+def turned_pair(x):
+    t = x.T
+    return jnp.concatenate([t[:BLOCK], t[BLOCK:]], axis=1)
+
+
+def add_products(index_ref, left, right_ref, acc, to, source, pair):
+    ens = acc.shape[2]
+    one = right_ref[index_ref[source, 2 * pair]]
+    two = right_ref[index_ref[source, 2 * pair + 1]]
+    out = jnp.dot(left, both(one, two), preferred_element_type=F32)
+    acc[index_ref[to, 2 * pair]] += out[:, :ens]
+    acc[index_ref[to, 2 * pair + 1]] += out[:, ens:]
+
+
+def forward_kernel(index_ref, raw, panels_ref, part_ref, turned_ref, pairs_ref, acc):
     acc[...] = jnp.zeros_like(acc)
-    ens = acc.shape[2]
-
-    def body(g, carry):
-        for j in range(PAIRS):
-            pair = g * PAIRS + j
-            one = right_ref[index_ref[source, 2 * pair]]
-            two = right_ref[index_ref[source, 2 * pair + 1]]
-            out = jnp.dot(left_ref[pair], both(one, two), preferred_element_type=F32)
-            acc[index_ref[to, 2 * pair]] += out[:, :ens]
-            acc[index_ref[to, 2 * pair + 1]] += out[:, ens:]
+    early = turned_ref.shape[0]
+
+    def body(turning, g, carry):
+        lower = lax.broadcasted_iota(jnp.int32, (BLOCK // 2, 2 * BLOCK), 1) < BLOCK
+        for sub in range(SUBS):
+            group = g * SUBS + sub
+            base = pl.multiple_of(group * SUB, SUB)
+            x = raw[pl.ds(base, SUB), :].reshape(SUB, BLOCK // 2, 2 * BLOCK)
+            for j in range(0, SUB, 2):
+                one, two = x[j], x[j + 1]
+                even = jnp.where(lower, one, halves_swapped(two))
+                odd = jnp.where(lower, halves_swapped(one), two)
+                left = jnp.concatenate([even, odd], axis=0)
+                pair = group * (SUB // 2) + j // 2
+                if turning:
+                    turned_ref[pair] = turned_pair(left)
+                else:
+                    pairs_ref[pair - early] = left
+                add_products(index_ref, left, panels_ref, acc, 0, 1, pair)
         return carry
 
-    lax.fori_loop(0, left_ref.shape[0] // PAIRS, body, 0)
-
-
-def forward_kernel(index_ref, pairs_ref, panels_ref, part_ref, acc):
-    products(index_ref, pairs_ref, panels_ref, acc, 0, 1)
+    each = SUBS * SUB // 2
+    lax.fori_loop(0, early // each, functools.partial(body, True), 0)
+    lax.fori_loop(early // each, raw.shape[0] // (2 * each), functools.partial(body, False), 0)
     part_ref[...] = acc[pl.ds(0, part_ref.shape[0])].astype(BF16)
 
 
 def exchange_kernel(
-    regions, part_ref, obs_ref, inv_ref, pairs_ref, all_ref, own_ref, turned_ref, got, send_a, recv_a, send_b, recv_b
+    regions, part_ref, obs_ref, inv_ref, pairs_ref, all_ref, own_ref, turned_ref, got, send_a, recv_a, send_b, recv_b, send_c, recv_c
 ):
     me = lax.axis_index("region")
     rows, ens = obs_ref.shape
@@ -231,14 +231,30 @@
             device_id_type=MESH,
         )
 
-    def second(k):
-        peer = lax.rem(me + k, regions)
+    width = 2 if regions % 2 == 0 else 1
+    count = regions // width
+    high, low = me // width, lax.rem(me, width)
+
+    def at(k, low):
+        return lax.rem(high + count - k, count) * width + low
+
+    def along(k, source):
         return pltpu.make_async_remote_copy(
-            src_ref=all_ref.at[me],
-            dst_ref=all_ref.at[me],
+            src_ref=all_ref.at[source],
+            dst_ref=all_ref.at[source],
             send_sem=send_b.at[k],
             recv_sem=recv_b.at[k],
-            device_id={"region": peer},
+            device_id={"region": lax.rem(high + k, count) * width + low},
+            device_id_type=MESH,
+        )
+
+    def across(k, source):
+        return pltpu.make_async_remote_copy(
+            src_ref=all_ref.at[source],
+            dst_ref=all_ref.at[source],
+            send_sem=send_c.at[k],
+            recv_sem=recv_c.at[k],
+            device_id={"region": high * width + 1 - low},
             device_id_type=MESH,
         )
 
@@ -250,43 +266,52 @@
 
     def turn(g, carry):
         for j in range(TURNS):
-            x = pairs_ref[g * TURNS + j]
-            stacked = jnp.concatenate([x, halves_swapped(x)], axis=0)
-            turned_ref[g * TURNS + j] = stacked.T[:BLOCK]
+            turned_ref[g * TURNS + j] = turned_pair(pairs_ref[g * TURNS + j])
         return carry
 
-    lax.fori_loop(0, pair_count // TURNS // 2, turn, 0)
+    rounds = pair_count // TURNS
+    lax.fori_loop(0, rounds // 2, turn, 0)
     evolved = part_ref[me].astype(F32)
     for k in range(1, regions):
         firsts[k - 1].wait_recv()
         evolved = evolved + got[k].astype(F32)
     misfit = (inv * (evolved - obs)).astype(BF16)
     all_ref[me] = misfit
-    seconds = [second(k) for k in range(1, regions)]
+    seconds = [along(k, me) for k in range(1, count)]
     for copy in seconds:
         copy.start()
+    if width == 2:
+        seconds.append(across(0, me))
+        seconds[-1].start()
     own_ref[...] = lax.dot_general(
         table, misfit, (((0,), (0,)), ((), ())), preferred_element_type=F32
     ).astype(BF16)
-    for copy in firsts:
+    lax.fori_loop(rounds // 2, rounds * 3 // 4, turn, 0)
+    for k in range(1, count):
+        along(k, at(k, low)).wait_recv()
+        if width == 2:
+            seconds.append(across(k, at(k, low)))
+            seconds[-1].start()
+    lax.fori_loop(rounds * 3 // 4, rounds, turn, 0)
+    if width == 2:
+        for k in range(count):
+            across(k, at(k, 1 - low)).wait_recv()
+    for copy in firsts + seconds:
         copy.wait_send()
-    lax.fori_loop(pair_count // TURNS // 2, pair_count // TURNS, turn, 0)
-    for k in range(1, regions):
-        source = lax.rem(me - k + regions, regions)
-        pltpu.make_async_remote_copy(
-            src_ref=all_ref.at[source],
-            dst_ref=all_ref.at[source],
-            send_sem=send_b.at[k],
-            recv_sem=recv_b.at[k],
-            device_id={"region": source},
-            device_id_type=MESH,
-        ).wait_recv()
-    for copy in seconds:
-        copy.wait_send()
-
-
-def adjoint_kernel(index_ref, turned_ref, misfit_ref, own_ref, acc, misfit_out):
-    products(index_ref, turned_ref, misfit_ref, acc, 2, 3)
+
+
+def adjoint_kernel(index_ref, early_ref, late_ref, misfit_ref, own_ref, acc, misfit_out):
+    acc[...] = jnp.zeros_like(acc)
+    early = early_ref.shape[0]
+
+    def body(left_ref, first, g, carry):
+        for j in range(PAIRS):
+            pair = g * PAIRS + j
+            add_products(index_ref, left_ref[pair], misfit_ref, acc, 2, 3, first + pair)
+        return carry
+
+    lax.fori_loop(0, early // PAIRS, functools.partial(body, early_ref, 0), 0)
+    lax.fori_loop(0, late_ref.shape[0] // PAIRS, functools.partial(body, late_ref, early), 0)
     misfit_out[...] = own_ref[...]
 
 
@@ -384,18 +409,17 @@
     own_blocks = rows // BLOCK
     window_blocks = own_blocks * regions
 
-    panels, pairs, index = pl.pallas_call(
+    panels, raw, index = pl.pallas_call(
         functools.partial(blend_kernel, window_blocks),
         out_shape=(
             jax.ShapeDtypeStruct((slices, cells, ens), BF16),
-            jax.ShapeDtypeStruct((slots // 2, BLOCK, 2 * BLOCK), BF16),
+            jax.ShapeDtypeStruct((slots, BLOCK * BLOCK), BF16),
             jax.ShapeDtypeStruct((4, slots), jnp.int32),
         ),
         in_specs=[hbm()] * 3 + [vmem()] + [hbm()] * 3,
         out_specs=(vmem(), vmem(), vmem()),
         scratch_shapes=[
             pltpu.VMEM((slices, cells, ens), BF16),
-            pltpu.VMEM((slots, BLOCK * BLOCK), BF16),
             pltpu.VMEM((slices, slices), F32),
             pltpu.VMEM((1, slots), jnp.int32),
             pltpu.VMEM((1, slots), jnp.int32),
@@ -419,22 +443,23 @@
     )
 
     smem = pl.BlockSpec(memory_space=pltpu.SMEM)
-    part = pl.pallas_call(
+    half = jax.ShapeDtypeStruct((slots // 4, BLOCK, 2 * BLOCK), BF16)
+    part, early, pairs = pl.pallas_call(
         forward_kernel,
-        out_shape=jax.ShapeDtypeStruct((window_blocks, BLOCK, ens), BF16),
+        out_shape=(jax.ShapeDtypeStruct((window_blocks, BLOCK, ens), BF16), half, half),
         in_specs=[smem, vmem(), vmem()],
-        out_specs=vmem(),
+        out_specs=(vmem(), vmem(), vmem()),
         scratch_shapes=[pltpu.VMEM((window_blocks + 1, BLOCK, ens), F32)],
         compiler_params=pltpu.CompilerParams(vmem_limit_bytes=16 << 20),
         name="forward_blocks",
-    )(index, pairs, panels.reshape(panel_total, BLOCK, ens))
-
-    misfit_all, own, turned = pl.pallas_call(
+    )(index, raw, panels.reshape(panel_total, BLOCK, ens))
+
+    misfit_all, own, late = pl.pallas_call(
         functools.partial(exchange_kernel, regions),
         out_shape=(
             jax.ShapeDtypeStruct((regions, rows, ens), BF16),
             jax.ShapeDtypeStruct((rows, ens), BF16),
-            jax.ShapeDtypeStruct((slots // 2, BLOCK, 2 * BLOCK), BF16),
+            half,
         ),
         in_specs=[vmem()] * 4,
         out_specs=(vmem(), vmem(), vmem()),
@@ -444,6 +469,8 @@
             pltpu.SemaphoreType.DMA((regions,)),
             pltpu.SemaphoreType.DMA((regions,)),
             pltpu.SemaphoreType.DMA((regions,)),
+            pltpu.SemaphoreType.DMA((regions,)),
+            pltpu.SemaphoreType.DMA((regions,)),
         ],
         compiler_params=pltpu.CompilerParams(collective_id=1, has_side_effects=True, vmem_limit_bytes=16 << 20),
         name="misfit_exchange",
@@ -455,11 +482,11 @@
             jax.ShapeDtypeStruct((panel_total + 1, BLOCK, ens), F32),
             jax.ShapeDtypeStruct((rows, ens), BF16),
         ),
-        in_specs=[smem, vmem(), vmem(), vmem()],
+        in_specs=[smem] + [vmem()] * 4,
         out_specs=(vmem(), vmem()),
         compiler_params=pltpu.CompilerParams(vmem_limit_bytes=16 << 20),
         name="adjoint_blocks",
-    )(index, turned, misfit_all.reshape(window_blocks, BLOCK, ens), own)
+    )(index, early, late, misfit_all.reshape(window_blocks, BLOCK, ens), own)
 
     blocks_shape = (cell_blocks, slabs, BLOCK, ens)
     gradient = pl.pallas_call(

time: 65.4 us -> 77.2 us (1.18)
  Pallas kernels: 62.9 us -> 74.4 us
    pallas_call x1, Pallas kernels: 10.6 us -> 30.4 us  [shards(): pl.pallas_call(forward_kernel, out_shape=(jax.ShapeDtypeStruct((window_bl...]
    pallas_call x1, Pallas kernels: 9.43 us -> 4.63 us  [shards(): pl.pallas_call(functools.partial(blend_kernel, window_blocks), out_shape=...]
    pallas_call x1, Pallas kernels: 25.6 us -> 22.7 us  [shards(): pl.pallas_call(functools.partial(exchange_kernel, regions), out_shape=(ja...]
where the time goes in v4:
time: 77.2 us; the launch traced here: 76.7 us
  Pallas kernels  74.4 us (96%)
  between operations  1.36 us (2%)
  local copies, waits for them, and re-layouts  1 us (1%)
    pallas_call x1, Pallas kernels, shards(): pl.pallas_call(forward_kernel, out_shape=(jax.ShapeDtypeStruct((window_bl...  30.4 us
    pallas_call x1, Pallas kernels, shards(): pl.pallas_call(functools.partial(exchange_kernel, regions), out_shape=(ja...  22.7 us
    pallas_call x1, Pallas kernels, shards(): pl.pallas_call(adjoint_kernel, out_shape=(jax.ShapeDtypeStruct((panel_tot...  11.1 us
    pallas_call x1, Pallas kernels, shards(): pl.pallas_call(gradient_kernel, out_shape=jax.ShapeDtypeStruct((slabs, ce...  5.55 us
    pallas_call x1, Pallas kernels, shards(): pl.pallas_call(functools.partial(blend_kernel, window_blocks), out_shape=...  4.63 us

profile of v4, /device:TPU:0, one launch (start us, length us, event | category | flops | bytes accessed | tf_op | source)
XLA Modules:
  0.0 76.7 jit_solution(11650239961095359830)
XLA Ops:
  1.3 4.6 %blend_slices.1 = (bf16[16,512,128]{2,1,0:T(8,128)(2,1)S(1)}, bf16[1024,4096]{1,0:T(8,128)(2,1)S(1)}, s32[4,1024]{1,0:T(4,128)S(1)}) custom-call(s32[1,1024]{1,0:T(1,128)} %recv_hbm.1, s32[1,1024]{1,0:T(1,128)} %cell_hbm.1, s32[1,1024]{1,0:T(1,128)} %slice_hbm.1, s32[1,1]{1,0:T(1,128)S(6)} %copy.13.live_ref, f32[16,16]{1,0:T(8,128)} %blend_ref.1, ...), custom_call_target="tpu_custom_call" | custom-call | tf_op jit(solution)/shard_map/blend_slices/pallas_call | solution.py:412
  5.9 0.0 copy-start
  5.9 0.0 copy-start.3
  5.9 30.4 %forward_blocks.1 = (bf16[16,64,128]{2,1,0:T(8,128)(2,1)S(1)}, bf16[256,64,128]{2,1,0:T(8,128)(2,1)S(1)}, bf16[256,64,128]{2,1,0:T(8,128)(2,1)S(1)}) custom-call(s32[4,1024]{1,0:T(4,128)S(1)} %get-tuple-element.13.index_ref, bf16[1024,4096]{1,0:T(8,128)(2,1)S(1)} %get-tuple-element.14.raw, bf16[128,64,128]{2,1,0:T(8,128)(2,1)S(1)} %bitcast.5), custom_call_target="tpu_custom_call" | custom-call | tf_op jit(solution)/shard_map/forward_blocks/pallas_call | solution.py:447
  36.3 0.0 copy-done
  36.4 0.0 copy-done.3
  36.4 22.7 %misfit_exchange.1 = (bf16[8,128,128]{2,1,0:T(8,128)(2,1)S(1)}, bf16[128,128]{1,0:T(8,128)(2,1)S(1)}, bf16[256,64,128]{2,1,0:T(8,128)(2,1)S(1)}) custom-call(bf16[8,128,128]{2,1,0:T(8,128)(2,1)S(1)} %bitcast.7, bf16[128,128]{1,0:T(8,128)(2,1)S(1)} %bitcast.8, f32[1,128]{1,0:T(1,128)S(1)} %copy-done.3, bf16[256,64,128]{2,1,0:T(8,128)(2,1)S(1)} %get-tuple-element.18.pairs_ref), custom_call_target="tpu_custom_call" | custom-call | tf_op jit(solution)/shard_map/misfit_exchange/pallas_call | solution.py:457
  59.0 0.0 copy-start.1
  59.0 0.0 copy-start.2
  59.1 11.1 %adjoint_blocks.1 = (f32[129,64,128]{2,1,0:T(8,128)S(1)}, bf16[128,128]{1,0:T(8,128)(2,1)}) custom-call(s32[4,1024]{1,0:T(4,128)S(1)} %get-tuple-element.13.index_ref, bf16[256,64,128]{2,1,0:T(8,128)(2,1)S(1)} %get-tuple-element.16.early_ref, bf16[256,64,128]{2,1,0:T(8,128)(2,1)S(1)} %get-tuple-element.19.late_ref, bf16[16,64,128]{2,1,0:T(8,128)(2,1)S(1)} %bitcast.6, ...), custom_call_target="tpu_custom_call" | custom-call | tf_op jit(solution)/shard_map/adjoint_blocks/pallas_call | solution.py:479
  70.2 0.0 copy-done.1
  70.2 0.0 copy-done.2
  70.2 5.6 %gradient_exchange.1 = bf16[8,512,128]{2,1,0:T(8,128)(2,1)S(1)} custom-call(f32[129,64,128]{2,1,0:T(8,128)S(1)} %get-tuple-element.23.acc_ref, f32[16,16]{1,0:T(8,128)S(1)} %copy-done.2, bf16[128,128]{1,0:T(8,128)(2,1)S(1)} %copy-done.1), custom_call_target="tpu_custom_call" | custom-call | tf_op jit(solution)/shard_map/gradient_exchange/pallas_call | solution.py:492
  75.8 1.0 %copy.14 = bf16[8,512,128]{2,1,0:T(8,128)(2,1)} copy(bf16[8,512,128]{2,1,0:T(8,128)(2,1)S(1)} %gradient_exchange.1) | data formatting | bytes 2097152
Async XLA Ops:
  5.9 30.4 %copy-start = (bf16[1,128,128]{2,1,0:T(8,128)(2,1)S(1)}, bf16[1,128,128]{2,1,0:T(8,128)(2,1)}, u32[]{:S(2)}) copy-start(bf16[1,128,128]{2,1,0:T(8,128)(2,1)} %param.17) | copy-start | bytes 98308
  5.9 30.4 %copy-start.3 = (f32[1,128]{1,0:T(1,128)S(1)}, f32[1,128]{1,0:T(1,128)}, u32[]{:S(2)}) copy-start(f32[1,128]{1,0:T(1,128)} %inv_ref.1) | copy-start | bytes 1540
  59.0 11.2 %copy-start.1 = (bf16[128,128]{1,0:T(8,128)(2,1)S(1)}, bf16[128,128]{1,0:T(8,128)(2,1)}, u32[]{:S(2)}) copy-start(bf16[128,128]{1,0:T(8,128)(2,1)} %mix_ref.1) | copy-start | bytes 98308
  59.0 11.2 %copy-start.2 = (f32[16,16]{1,0:T(8,128)S(1)}, f32[16,16]{1,0:T(8,128)}, u32[]{:S(2)}) copy-start(f32[16,16]{1,0:T(8,128)} %blend_ref.1) | copy-start | bytes 3076

commit v5 on v3

--- a/solution.py
+++ b/solution.py
@@ -201,8 +201,13 @@
     part_ref[...] = acc[pl.ds(0, part_ref.shape[0])].astype(BF16)
 
 
+def turned_pair(x):
+    t = x.T
+    return jnp.concatenate([t[:BLOCK], t[BLOCK:]], axis=1)
+
+
 def exchange_kernel(
-    regions, part_ref, obs_ref, inv_ref, pairs_ref, all_ref, own_ref, turned_ref, got, send_a, recv_a, send_b, recv_b
+    regions, part_ref, obs_ref, inv_ref, pairs_ref, all_ref, own_ref, turned_ref, got, send_a, recv_a, send_b, recv_b, send_c, recv_c
 ):
     me = lax.axis_index("region")
     rows, ens = obs_ref.shape
@@ -231,14 +236,30 @@
             device_id_type=MESH,
         )
 
-    def second(k):
-        peer = lax.rem(me + k, regions)
+    width = 2 if regions % 2 == 0 else 1
+    count = regions // width
+    high, low = me // width, lax.rem(me, width)
+
+    def at(k, low):
+        return lax.rem(high + count - k, count) * width + low
+
+    def along(k, source):
         return pltpu.make_async_remote_copy(
-            src_ref=all_ref.at[me],
-            dst_ref=all_ref.at[me],
+            src_ref=all_ref.at[source],
+            dst_ref=all_ref.at[source],
             send_sem=send_b.at[k],
             recv_sem=recv_b.at[k],
-            device_id={"region": peer},
+            device_id={"region": lax.rem(high + k, count) * width + low},
+            device_id_type=MESH,
+        )
+
+    def across(k, source):
+        return pltpu.make_async_remote_copy(
+            src_ref=all_ref.at[source],
+            dst_ref=all_ref.at[source],
+            send_sem=send_c.at[k],
+            recv_sem=recv_c.at[k],
+            device_id={"region": high * width + 1 - low},
             device_id_type=MESH,
         )
 
@@ -250,38 +271,37 @@
 
     def turn(g, carry):
         for j in range(TURNS):
-            x = pairs_ref[g * TURNS + j]
-            stacked = jnp.concatenate([x, halves_swapped(x)], axis=0)
-            turned_ref[g * TURNS + j] = stacked.T[:BLOCK]
+            turned_ref[g * TURNS + j] = turned_pair(pairs_ref[g * TURNS + j])
         return carry
 
-    lax.fori_loop(0, pair_count // TURNS // 2, turn, 0)
+    rounds = pair_count // TURNS
+    lax.fori_loop(0, rounds // 2, turn, 0)
     evolved = part_ref[me].astype(F32)
     for k in range(1, regions):
         firsts[k - 1].wait_recv()
         evolved = evolved + got[k].astype(F32)
     misfit = (inv * (evolved - obs)).astype(BF16)
     all_ref[me] = misfit
-    seconds = [second(k) for k in range(1, regions)]
+    seconds = [along(k, me) for k in range(1, count)]
     for copy in seconds:
         copy.start()
+    if width == 2:
+        seconds.append(across(0, me))
+        seconds[-1].start()
     own_ref[...] = lax.dot_general(
         table, misfit, (((0,), (0,)), ((), ())), preferred_element_type=F32
     ).astype(BF16)
-    for copy in firsts:
-        copy.wait_send()
-    lax.fori_loop(pair_count // TURNS // 2, pair_count // TURNS, turn, 0)
-    for k in range(1, regions):
-        source = lax.rem(me - k + regions, regions)
-        pltpu.make_async_remote_copy(
-            src_ref=all_ref.at[source],
-            dst_ref=all_ref.at[source],
-            send_sem=send_b.at[k],
-            recv_sem=recv_b.at[k],
-            device_id={"region": source},
-            device_id_type=MESH,
-        ).wait_recv()
-    for copy in seconds:
+    lax.fori_loop(rounds // 2, rounds * 3 // 4, turn, 0)
+    for k in range(1, count):
+        along(k, at(k, low)).wait_recv()
+        if width == 2:
+            seconds.append(across(k, at(k, low)))
+            seconds[-1].start()
+    lax.fori_loop(rounds * 3 // 4, rounds, turn, 0)
+    if width == 2:
+        for k in range(count):
+            across(k, at(k, 1 - low)).wait_recv()
+    for copy in firsts + seconds:
         copy.wait_send()
 
 
@@ -444,6 +464,8 @@
             pltpu.SemaphoreType.DMA((regions,)),
             pltpu.SemaphoreType.DMA((regions,)),
             pltpu.SemaphoreType.DMA((regions,)),
+            pltpu.SemaphoreType.DMA((regions,)),
+            pltpu.SemaphoreType.DMA((regions,)),
         ],
         compiler_params=pltpu.CompilerParams(collective_id=1, has_side_effects=True, vmem_limit_bytes=16 << 20),
         name="misfit_exchange",

time: 65.4 us -> 62 us (0.948)
  Pallas kernels: 62.9 us -> 59.7 us
    pallas_call x1, Pallas kernels: 25.6 us -> 22.1 us  [shards(): pl.pallas_call(functools.partial(exchange_kernel, regions), out_shape=(ja...]
where the time goes in v5:
time: 62 us; the launch traced here: 62.1 us
  Pallas kernels  59.7 us (96%)
  between operations  1.36 us (2%)
  local copies, waits for them, and re-layouts  0.99 us (2%)
    pallas_call x1, Pallas kernels, shards(): pl.pallas_call(functools.partial(exchange_kernel, regions), out_shape=(ja...  22.1 us
    pallas_call x1, Pallas kernels, shards(): pl.pallas_call(adjoint_kernel, out_shape=(jax.ShapeDtypeStruct((panel_tot...  11.8 us
    pallas_call x1, Pallas kernels, shards(): pl.pallas_call(forward_kernel, out_shape=jax.ShapeDtypeStruct((window_blo...  10.8 us
    pallas_call x1, Pallas kernels, shards(): pl.pallas_call(functools.partial(blend_kernel, window_blocks), out_shape=...  9.43 us
    pallas_call x1, Pallas kernels, shards(): pl.pallas_call(gradient_kernel, out_shape=jax.ShapeDtypeStruct((slabs, ce...  5.6 us

profile of v5, /device:TPU:0, one launch (start us, length us, event | category | flops | bytes accessed | tf_op | source)
XLA Modules:
  0.0 62.1 jit_solution(14139846048089698845)
XLA Ops:
  1.3 0.0 copy-start
  1.3 0.0 copy-start.3
  1.3 9.4 %blend_slices.1 = (bf16[16,512,128]{2,1,0:T(8,128)(2,1)S(1)}, bf16[512,64,128]{2,1,0:T(8,128)(2,1)S(1)}, s32[4,1024]{1,0:T(4,128)S(1)}) custom-call(s32[1,1024]{1,0:T(1,128)} %recv_hbm.1, s32[1,1024]{1,0:T(1,128)} %cell_hbm.1, s32[1,1024]{1,0:T(1,128)} %slice_hbm.1, s32[1,1]{1,0:T(1,128)S(6)} %copy.13.live_ref, f32[16,16]{1,0:T(8,128)} %blend_ref.1, ...), custom_call_target="tpu_custom_call" | custom-call | tf_op jit(solution)/shard_map/blend_slices/pallas_call | solution.py:407
  10.7 10.8 %forward_blocks.1 = bf16[16,64,128]{2,1,0:T(8,128)(2,1)S(1)} custom-call(s32[4,1024]{1,0:T(4,128)S(1)} %get-tuple-element.10.index_ref, bf16[512,64,128]{2,1,0:T(8,128)(2,1)S(1)} %get-tuple-element.11.pairs_ref, bf16[128,64,128]{2,1,0:T(8,128)(2,1)S(1)} %bitcast.5), custom_call_target="tpu_custom_call" | custom-call | tf_op jit(solution)/shard_map/forward_blocks/pallas_call | solution.py:442
  21.5 0.0 copy-done
  21.5 0.0 copy-done.3
  21.5 0.0 copy-start.1
  21.5 0.0 copy-start.2
  21.6 22.1 %misfit_exchange.1 = (bf16[8,128,128]{2,1,0:T(8,128)(2,1)S(1)}, bf16[128,128]{1,0:T(8,128)(2,1)S(1)}, bf16[512,64,128]{2,1,0:T(8,128)(2,1)S(1)}) custom-call(bf16[8,128,128]{2,1,0:T(8,128)(2,1)S(1)} %bitcast.6, bf16[128,128]{1,0:T(8,128)(2,1)S(1)} %bitcast.8, f32[1,128]{1,0:T(1,128)S(1)} %copy-done.3, bf16[512,64,128]{2,1,0:T(8,128)(2,1)S(1)} %get-tuple-element.11.pairs_ref), custom_call_target="tpu_custom_call" | custom-call | tf_op jit(solution)/shard_map/misfit_exchange/pallas_call | solution.py:452
  43.6 11.8 %adjoint_blocks.1 = (f32[129,64,128]{2,1,0:T(8,128)S(1)}, bf16[128,128]{1,0:T(8,128)(2,1)}) custom-call(s32[4,1024]{1,0:T(4,128)S(1)} %get-tuple-element.10.index_ref, bf16[512,64,128]{2,1,0:T(8,128)(2,1)S(1)} %get-tuple-element.13.turned_ref, bf16[16,64,128]{2,1,0:T(8,128)(2,1)S(1)} %bitcast.7, bf16[128,128]{1,0:T(8,128)(2,1)S(1)} %get-tuple-element.15.own_ref), custom_call_target="tpu_custom_call" | custom-call | tf_op jit(solution)/shard_map/adjoint_blocks/pallas_call | solution.py:474
  55.5 0.0 copy-done.1
  55.5 0.0 copy-done.2
  55.5 5.6 %gradient_exchange.1 = bf16[8,512,128]{2,1,0:T(8,128)(2,1)S(1)} custom-call(f32[129,64,128]{2,1,0:T(8,128)S(1)} %get-tuple-element.17.acc_ref, f32[16,16]{1,0:T(8,128)S(1)} %copy-done.2, bf16[128,128]{1,0:T(8,128)(2,1)S(1)} %copy-done.1), custom_call_target="tpu_custom_call" | custom-call | tf_op jit(solution)/shard_map/gradient_exchange/pallas_call | solution.py:487
  61.1 1.0 %copy.14 = bf16[8,512,128]{2,1,0:T(8,128)(2,1)} copy(bf16[8,512,128]{2,1,0:T(8,128)(2,1)S(1)} %gradient_exchange.1) | data formatting | bytes 2097152
Async XLA Ops:
  1.3 20.2 %copy-start = (bf16[1,128,128]{2,1,0:T(8,128)(2,1)S(1)}, bf16[1,128,128]{2,1,0:T(8,128)(2,1)}, u32[]{:S(2)}) copy-start(bf16[1,128,128]{2,1,0:T(8,128)(2,1)} %param.17) | copy-start | bytes 98308
  1.3 20.2 %copy-start.3 = (f32[1,128]{1,0:T(1,128)S(1)}, f32[1,128]{1,0:T(1,128)}, u32[]{:S(2)}) copy-start(f32[1,128]{1,0:T(1,128)} %inv_ref.1) | copy-start | bytes 1540
  21.5 34.0 %copy-start.1 = (bf16[128,128]{1,0:T(8,128)(2,1)S(1)}, bf16[128,128]{1,0:T(8,128)(2,1)}, u32[]{:S(2)}) copy-start(bf16[128,128]{1,0:T(8,128)(2,1)} %mix_ref.1) | copy-start | bytes 98308
  21.5 33.9 %copy-start.2 = (f32[16,16]{1,0:T(8,128)S(1)}, f32[16,16]{1,0:T(8,128)}, u32[]{:S(2)}) copy-start(f32[16,16]{1,0:T(8,128)} %blend_ref.1) | copy-start | bytes 3076
